TPU v7x, 32 devices: a whole 2x2x4 slice. The times are simulated.
32 devices in a mesh: ta: 4 (over x, core), ha: 4 (over z), wa: 2 (over y).
Axes of the slice: x: 2, y: 2, z: 4, core: 2. Of those that a mesh axis runs over, the one named last changes fastest.
Arguments:
- tokens: bfloat16 [1, 16, 32, 16, 1024], P(None, 'ta', 'ha', 'wa'), may hold values from -40 to 40
- norm_gain: float32 [4, 1024], replicated, may hold values from 0.25 to 1.75
- qkv_weight: bfloat16 [3, 1024, 3, 1024], P(None, None, None, 'ta'), may hold values from -0.1875 to 0.1875
- qk_gain: float32 [3, 2, 64], replicated, may hold values from 0.25 to 1.75
- out_weight: bfloat16 [3, 1024, 1024], P(None, 'ta'), may hold values from -0.1875 to 0.1875
- ffn_in: bfloat16 [1024, 2, 2048], P(None, None, 'ta'), may hold values from -0.1875 to 0.1875
- ffn_out: bfloat16 [2048, 1024], P('ta'), may hold values from -0.125 to 0.125
Outputs:
- layer_out: bfloat16 [1, 16, 32, 16, 1024], P(None, 'ta', 'ha', 'wa')
All inputs are finite; a program needn't handle non-finite values.
Results may differ from a plain program's by a relative error of at most 0.015.
Values may be sent and summed in bfloat16 or wider, within the bound.
No kernel may reach another device: no remote copies, remote signals or barrier semaphores. Data moves between devices by JAX's collectives and lax.ppermute only.
A program may use at most 192 MiB of HBM per device.

v0:
```python
import functools
import math

import jax
import jax.numpy as jnp
from jax import lax
from jax.experimental import pallas as pl
from jax.experimental.pallas import tpu as pltpu
from jax.sharding import PartitionSpec as P

HEAD_DIM = 64
GROUP = 128
F32 = jnp.float32
BF16 = jnp.bfloat16


def vmem():
    return pl.BlockSpec(memory_space=pltpu.VMEM)


def smem():
    return pl.BlockSpec(memory_space=pltpu.SMEM)


def call(body, outs, in_specs, scratch=()):
    return pl.pallas_call(
        body,
        out_shape=outs,
        in_specs=in_specs,
        out_specs=jax.tree.map(lambda _: vmem(), outs),
        scratch_shapes=list(scratch),
        compiler_params=pltpu.CompilerParams(vmem_limit_bytes=48 * 1024 * 1024),
    )


def rms(stream, gain):
    return (
        stream * lax.rsqrt(jnp.mean(stream * stream, axis=-1, keepdims=True) + 1e-06) * gain
    ).astype(BF16)


def norm_tokens(stream, gain):
    def body(x_ref, g_ref, o_ref):
        o_ref[...] = rms(x_ref[...].astype(F32), g_ref[...])

    out = jax.ShapeDtypeStruct(stream.shape, BF16)
    return call(body, out, [vmem(), vmem()])(stream, gain)


def attention(pieces, weight, gains, place, frames, line, stride, causal):
    count = len(pieces)
    rows, width = pieces[0].shape
    local = weight.shape[1] // 3
    heads = local // HEAD_DIM
    spots = rows // frames

    def body(*refs):
        g_ref = refs[0]
        x_refs = refs[1 : 1 + count]
        w_ref, gain_ref = refs[1 + count : 3 + count]
        o_refs = refs[3 + count : 3 + 2 * count]
        q_s, k_s, v_s, o_s = refs[3 + 2 * count :]
        lane_head = lax.broadcasted_iota(jnp.int32, (local, local), 0) // HEAD_DIM
        same_head = lane_head == lax.broadcasted_iota(jnp.int32, (local, local), 1) // HEAD_DIM
        ones = jnp.where(same_head, 1.0, 0.0).astype(BF16)

        def head_norm(v, gain):
            sq = v * v
            high = sq.astype(BF16)
            low = (sq - high.astype(F32)).astype(BF16)
            total = jnp.dot(high, ones, preferred_element_type=F32) + jnp.dot(
                low, ones, preferred_element_type=F32
            )
            return v * lax.rsqrt(total * (1.0 / HEAD_DIM) + 1e-06) * gain

        for r in range(count):
            qkv = jnp.dot(x_refs[r][...], w_ref[...], preferred_element_type=F32)
            shape = (frames, spots, local)
            at = slice(r * frames, (r + 1) * frames)
            q_s[at] = head_norm(qkv[:, :local], gain_ref[0:1]).reshape(shape)
            k_s[at] = head_norm(qkv[:, local : 2 * local], gain_ref[1:2]).reshape(shape)
            v_s[at] = qkv[:, 2 * local :].reshape(shape)

        q_at = lax.broadcasted_iota(jnp.int32, (heads * GROUP, GROUP), 0) % GROUP
        k_at = lax.broadcasted_iota(jnp.int32, (heads * GROUP, GROUP), 1)
        all_frames = count * frames
        if causal:
            per = GROUP // all_frames

            def frame_of(at):
                f = at // per
                return (g_ref[0] ^ (f // frames)) * frames + f % frames

            allowed = (q_at % per == k_at % per) & (frame_of(k_at) <= frame_of(q_at))
            groups = spots // per
        else:
            full = line * stride

            def line_of(at):
                return (at // full) * stride + at % stride

            allowed = line_of(q_at) == line_of(k_at)
            groups = count * rows // GROUP
        own_head = lax.broadcasted_iota(jnp.int32, (GROUP, local), 1) // HEAD_DIM
        for c in range(groups):
            if causal:
                where = (slice(None), slice(c * per, (c + 1) * per), slice(None))
            elif spots >= GROUP:
                f, s = divmod(c * GROUP, spots)
                where = (slice(f, f + 1), slice(s, s + GROUP), slice(None))
            else:
                some = GROUP // spots
                where = (slice(c * some, (c + 1) * some), slice(None), slice(None))
            q = q_s[where].reshape(GROUP, local).astype(BF16)
            k = k_s[where].reshape(GROUP, local).astype(BF16)
            v = v_s[where].reshape(GROUP, local).astype(BF16)
            stacked = jnp.concatenate(
                [jnp.where(own_head == h, q, jnp.zeros_like(q)) for h in range(heads)], axis=0
            )
            scores = lax.dot_general(
                stacked, k, (((1,), (1,)), ((), ())), preferred_element_type=F32
            ) * (1.0 / math.sqrt(HEAD_DIM))
            weights = jnp.where(allowed, jnp.exp(scores), 0.0)
            probs = (weights / jnp.sum(weights, axis=-1, keepdims=True)).astype(BF16)
            mixed = jnp.dot(probs, v, preferred_element_type=F32)
            out = mixed[:GROUP]
            for h in range(1, heads):
                out = jnp.where(own_head == h, mixed[h * GROUP : (h + 1) * GROUP], out)
            o_s[where] = out.reshape(o_s[where].shape)
        for r in range(count):
            at = slice(r * frames, (r + 1) * frames)
            o_refs[r][...] = o_s[at].reshape(rows, local).astype(BF16)

    outs = [jax.ShapeDtypeStruct((rows, local), BF16)] * count
    scratch = [pltpu.VMEM((count * frames, spots, local), F32)] * 4
    return call(body, outs, [smem()] + [vmem()] * (count + 2), scratch)(
        place, *pieces, weight, gains
    )


def out_product(pieces, weight, stream, gain, place, keep):
    count = len(pieces)

    def body(*refs):
        g_ref = refs[0]
        x_refs = refs[1 : 1 + count]
        w_ref, s_ref, gain_ref = refs[1 + count : 4 + count]
        total = s_ref[...].astype(F32)
        for r in range(count):
            total = total + jnp.dot(
                x_refs[r][...], w_ref[g_ref[0] ^ r], preferred_element_type=F32
            )
        refs[4 + count][...] = total.astype(keep)
        if gain is not None:
            refs[5 + count][...] = rms(total, gain_ref[...])

    outs = [jax.ShapeDtypeStruct(stream.shape, keep)]
    if gain is not None:
        outs.append(jax.ShapeDtypeStruct(stream.shape, BF16))
    spare = jnp.ones((1, stream.shape[1]), F32) if gain is None else gain
    return call(body, outs, [smem()] + [vmem()] * (count + 3))(
        place, *pieces, weight, stream, spare
    )


def mlp_hidden(pieces, weight):
    count = len(pieces)
    rows = pieces[0].shape[0]
    units = weight.shape[1] // 2

    def body(*refs):
        w_ref = refs[count]
        for r in range(count):
            both = jnp.dot(refs[r][...], w_ref[...], preferred_element_type=F32)
            gate = both[:, :units]
            refs[count + 1 + r][...] = (
                gate / (1.0 + jnp.exp(-gate)) * both[:, units:]
            ).astype(BF16)

    outs = [jax.ShapeDtypeStruct((rows, units), BF16)] * count
    return call(body, outs, [vmem()] * (count + 1))(*pieces, weight)


def flip(x, size, by):
    return lax.ppermute(x, "ta", [(i, i ^ by) for i in range(size)])


def spread(own, size):
    pieces = {0: own}
    half = size // 2
    while half:
        for r in list(pieces):
            pieces[r ^ half] = flip(pieces[r], size, half)
        half //= 2
    return [pieces[r] for r in range(size)]


def exchange(pieces):
    size = len(pieces)
    return [pieces[0]] + [flip(pieces[r], size, r) for r in range(1, size)]


def local(sizes, tokens, norm_gain, qkv_weight, qk_gain, out_weight, ffn_in, ffn_out):
    ta, ha, wa = sizes
    clips, frames, rows, cols, width = tokens.shape
    place = lax.axis_index("ta").astype(jnp.int32).reshape(1)
    count = clips * frames * rows * cols
    head_count = qkv_weight.shape[-1] // HEAD_DIM
    gains = jnp.tile(qk_gain, (1, 1, head_count))
    whole_out = [lax.all_gather(out_weight[p], "ta", axis=0) for p in range(3)]
    whole_down = lax.all_gather(ffn_out, "ta", axis=0)
    norms = norm_gain[:, None, :]

    def attend(normed, p, line, stride, causal):
        weight = qkv_weight[p].reshape(width, -1)
        pieces = spread(normed, ta)
        return exchange(
            attention(pieces, weight, gains[p], place, frames, line, stride, causal)
        )

    stream = lax.all_to_all(tokens, "wa", split_axis=2, concat_axis=3, tiled=True)
    stream = stream.reshape(count, width)
    normed = norm_tokens(stream, norms[0])
    got = attend(normed, 0, cols * wa, 1, False)
    (stream,) = out_product(got, whole_out[0], stream, None, place, BF16)

    few = cols // ha
    stream = stream.reshape(frames, rows // wa, wa, ha, few, width)
    stream = stream.transpose(3, 2, 0, 1, 4, 5).reshape(ha * wa, frames, rows // wa, few, width)
    stream = lax.all_to_all(stream, ("ha", "wa"), split_axis=0, concat_axis=0, tiled=True)
    stream = stream.transpose(1, 0, 2, 3, 4).reshape(count, width)

    normed = norm_tokens(stream, norms[1])
    got = attend(normed, 1, rows * ha, few, False)
    stream, normed = out_product(got, whole_out[1], stream, norms[2], place, F32)
    got = attend(normed, 2, frames * ta, 1, True)
    stream, normed = out_product(got, whole_out[2], stream, norms[3], place, F32)
    hidden = exchange(mlp_hidden(spread(normed, ta), ffn_in.reshape(width, -1)))
    (out,) = out_product(hidden, whole_down, stream, None, place, BF16)
    out = out.reshape(clips, frames, rows * ha, few, width)
    return lax.all_to_all(out, "ha", split_axis=2, concat_axis=3, tiled=True)


def solution(mesh):
    sizes = (mesh.shape["ta"], mesh.shape["ha"], mesh.shape["wa"])
    return jax.shard_map(
        functools.partial(local, sizes),
        mesh=mesh,
        in_specs=(
            P(None, "ta", "ha", "wa", None),
            P(),
            P(None, None, None, "ta"),
            P(),
            P(None, "ta", None),
            P(None, None, "ta"),
            P("ta", None),
        ),
        out_specs=P(None, "ta", "ha", "wa", None),
        check_vma=False,
    )
```

profile of v0, /device:TPU:0, one launch (start us, length us, event | category | flops | bytes accessed | tf_op | source)
XLA Modules:
  0.0 234.5 jit_solution(13375045053332562979)
XLA Ops:
  6.5 2.5 %fusion.1 = (bf16[1,256,1024]{2,1,0:T(8,128)(2,1)}, bf16[1,256,1024]{2,1,0:T(8,128)(2,1)}, bf16[1,256,1024]{2,1,0:T(8,128)(2,1)}) fusion(bf16[3,256,1024]{2,1,0:T(8,128)(2,1)} %param.11), kind=kLoop, calls=%fused_computation.4 | loop fusion | bytes 3145728 | tf_op jit(solution)/shard_map/slice | solution.py:210
  9.1 0.7 all-gather.8.cloned.1.call-update
  9.9 0.7 all-gather.10.cloned.1.call-update
  10.6 0.5 all-gather.12.cloned.1.call-update
  11.2 0.8 copy.23
  12.0 4.3 %all-to-all-start = ((bf16[1,4,8,8,1024]{4,3,1,0,2:T(8,128)(2,1)}), bf16[1,4,8,8,1024]{4,3,1,0,2:T(8,128)(2,1)S(1)}, u32[]{:S(2)}, u32[]{:S(2)}) async-start(bf16[1,4,8,8,1024]{4,3,1,0,2:T(8,128)(2,1)} %copy.23), calls=%async_computation | async-start | bytes 1048576 | tf_op jit(solution)/shard_map/all_to_all | solution.py:221
  16.3 8.7 %all-to-all-done = bf16[1,4,8,8,1024]{4,3,1,0,2:T(8,128)(2,1)S(1)} async-done(((bf16[1,4,8,8,1024]{4,3,1,0,2:T(8,128)(2,1)}), bf16[1,4,8,8,1024]{4,3,1,0,2:T(8,128)(2,1)S(1)}, u32[]{:S(2)}, u32[]{:S(2)}) %all-to-all-start) | async-done | bytes 524320 | tf_op jit(solution)/shard_map/all_to_all | solution.py:221
  25.3 1.8 collective-permute-start.1
  27.1 17.2 %collective-permute-done.1.refs_3_ = bf16[256,1024]{1,0:T(8,128)(2,1)S(1)} collective-permute-done((bf16[256,1024]{1,0:T(8,128)(2,1)S(1)}, bf16[256,1024]{1,0:T(8,128)(2,1)S(1)}, u32[]{:S(2)}, u32[]{:S(2)}) %collective-permute-start.1) | collective-permute-done | bytes 524320 | tf_op jit(solution)/shard_map/ppermute | solution.py:185
  44.2 4.4 %fusion = (bf16[1,1024,3,256]{3,1,2,0:T(8,128)(2,1)}, bf16[1,1024,3,256]{3,1,2,0:T(8,128)(2,1)}, bf16[1,1024,3,256]{3,1,2,0:T(8,128)(2,1)S(1)}) fusion(bf16[3,1024,3,256]{3,1,2,0:T(8,128)(2,1)} %param.9), kind=kLoop, calls=%fused_computation.3 | loop fusion | bytes 9437184 | tf_op jit(solution)/shard_map/slice | solution.py:215
  48.6 1.8 copy.35
  50.4 1.7 copy.26.refs_5_
  52.2 0.6 slice_bitcast_fusion
  52.8 4.9 %shard_map.74 = (bf16[256,256]{1,0:T(8,128)(2,1)S(1)}, bf16[256,256]{1,0:T(8,128)(2,1)S(1)}, bf16[256,256]{1,0:T(8,128)(2,1)S(1)}, bf16[256,256]{1,0:T(8,128)(2,1)S(1)}) custom-call(s32[1]{0:T(128)} %bitcast.refs_0_, bf16[256,1024]{1,0:T(8,128)(2,1)S(1)} %shard_map.73.refs_1_, bf16[256,1024]{1,0:T(8,128)(2,1)} %collective-permute-done.refs_2_, ...), custom_call_target="tpu_custom_call" | custom-call | tf_op jit(solution)/shard_map/pallas_call | solution.py:136
  57.7 0.6 collective-permute-start.3
  58.3 0.6 collective-permute-start.4
  58.9 0.9 collective-permute-start.5
  59.7 6.6 %collective-permute-done.4.refs_3_ = bf16[256,256]{1,0:T(8,128)(2,1)S(1)} collective-permute-done((bf16[256,256]{1,0:T(8,128)(2,1)S(1)}, bf16[256,256]{1,0:T(8,128)(2,1)S(1)}, u32[]{:S(2)}, u32[]{:S(2)}) %collective-permute-start.4) | collective-permute-done | bytes 131104 | tf_op jit(solution)/shard_map/ppermute | solution.py:185
  66.3 2.3 collective-permute-done.5.refs_4_
  68.6 1.6 copy-done.2
  70.2 0.7 shard_map.75
  71.1 0.5 copy.27
  71.7 20.1 %all_to_all.38 = bf16[8,4,4,2,1024]{4,3,2,1,0:T(2,128)(2,1)S(1)} all-to-all(bf16[8,4,4,2,1024]{4,3,2,1,0:T(2,128)(2,1)S(1)} %bitcast.33), channel_id=1, replica_groups=mesh['ta'=4,'ha'=4,'wa'=2] {'ha','wa'}, dimensions={0} | all-to-all | bytes 1048576 | tf_op jit(solution)/shard_map/all_to_all | solution.py:230
  91.8 0.5 copy.28
  92.5 0.2 shard_map.76.refs_1_
  92.7 0.6 collective-permute-start.7
  93.3 16.5 %collective-permute-done.7.refs_3_ = bf16[256,1024]{1,0:T(8,128)(2,1)S(1)} collective-permute-done((bf16[256,1024]{1,0:T(8,128)(2,1)S(1)}, bf16[256,1024]{1,0:T(8,128)(2,1)S(1)}, u32[]{:S(2)}, u32[]{:S(2)}) %collective-permute-start.7) | collective-permute-done | bytes 524320 | tf_op jit(solution)/shard_map/ppermute | solution.py:185
  109.8 1.8 copy.36
  111.5 1.7 copy.30.refs_5_
  113.4 5.3 %shard_map.77 = (bf16[256,256]{1,0:T(8,128)(2,1)S(1)}, bf16[256,256]{1,0:T(8,128)(2,1)S(1)}, bf16[256,256]{1,0:T(8,128)(2,1)}, bf16[256,256]{1,0:T(8,128)(2,1)S(1)}) custom-call(s32[1]{0:T(128)} %bitcast.refs_0_, bf16[256,1024]{1,0:T(8,128)(2,1)S(1)} %shard_map.76.refs_1_, bf16[256,1024]{1,0:T(8,128)(2,1)} %collective-permute-done.6.refs_2_, ...), custom_call_target="tpu_custom_call" | custom-call | tf_op jit(solution)/shard_map/pallas_call | solution.py:136
  118.6 0.8 collective-permute-start.10
  119.5 1.0 collective-permute-start.11
  120.5 0.3 collective-permute-start.9
  120.8 7.2 %collective-permute-done.10.refs_3_ = bf16[256,256]{1,0:T(8,128)(2,1)S(1)} collective-permute-done((bf16[256,256]{1,0:T(8,128)(2,1)}, bf16[256,256]{1,0:T(8,128)(2,1)S(1)}, u32[]{:S(2)}, u32[]{:S(2)}) %collective-permute-start.10) | collective-permute-done | bytes 131104 | tf_op jit(solution)/shard_map/ppermute | solution.py:185
  128.0 5.2 %collective-permute-done.11.refs_4_ = bf16[256,256]{1,0:T(8,128)(2,1)S(1)} collective-permute-done((bf16[256,256]{1,0:T(8,128)(2,1)S(1)}, bf16[256,256]{1,0:T(8,128)(2,1)S(1)}, u32[]{:S(2)}, u32[]{:S(2)}) %collective-permute-start.11) | collective-permute-done | bytes 131104 | tf_op jit(solution)/shard_map/ppermute | solution.py:185
  133.2 1.6 copy-done.1
  134.8 1.6 shard_map.78
  136.4 0.7 collective-permute-start.13
  137.2 13.8 %collective-permute-done.13.refs_3_ = bf16[256,1024]{1,0:T(8,128)(2,1)S(1)} collective-permute-done((bf16[256,1024]{1,0:T(8,128)(2,1)}, bf16[256,1024]{1,0:T(8,128)(2,1)S(1)}, u32[]{:S(2)}, u32[]{:S(2)}) %collective-permute-start.13) | collective-permute-done | bytes 524320 | tf_op jit(solution)/shard_map/ppermute | solution.py:185
  151.0 2.6 %copy.37 = bf16[1,1024,3,256]{1,3,2,0:T(8,128)(2,1)} copy(bf16[1,1024,3,256]{3,1,2,0:T(8,128)(2,1)} %get-tuple-element.45) | data formatting | bytes 3145728
  153.6 1.9 copy.32.refs_5_
  155.6 5.9 %shard_map.79 = (bf16[256,256]{1,0:T(8,128)(2,1)S(1)}, bf16[256,256]{1,0:T(8,128)(2,1)}, bf16[256,256]{1,0:T(8,128)(2,1)S(1)}, bf16[256,256]{1,0:T(8,128)(2,1)S(1)}) custom-call(s32[1]{0:T(128)} %bitcast.refs_0_, bf16[256,1024]{1,0:T(8,128)(2,1)} %get-tuple-element.33.refs_1_, bf16[256,1024]{1,0:T(8,128)(2,1)} %collective-permute-done.12.refs_2_, ...), custom_call_target="tpu_custom_call" | custom-call | tf_op jit(solution)/shard_map/pallas_call | solution.py:136
  161.5 0.5 collective-permute-start.15
  162.0 0.4 collective-permute-start.16
  162.4 1.0 collective-permute-start.17
  163.4 5.0 %collective-permute-done.16.refs_3_ = bf16[256,256]{1,0:T(8,128)(2,1)S(1)} collective-permute-done((bf16[256,256]{1,0:T(8,128)(2,1)S(1)}, bf16[256,256]{1,0:T(8,128)(2,1)S(1)}, u32[]{:S(2)}, u32[]{:S(2)}) %collective-permute-start.16) | collective-permute-done | bytes 131104 | tf_op jit(solution)/shard_map/ppermute | solution.py:185
  168.4 0.9 collective-permute-done.17.refs_4_
  169.3 1.6 copy-done
  170.9 0.8 shard_map.80
  171.7 0.6 collective-permute-start.19
  172.4 0.3 collective-permute-start.18
  172.6 13.7 %collective-permute-done.19.refs_2_ = bf16[256,1024]{1,0:T(8,128)(2,1)S(1)} collective-permute-done((bf16[256,1024]{1,0:T(8,128)(2,1)S(1)}, bf16[256,1024]{1,0:T(8,128)(2,1)S(1)}, u32[]{:S(2)}, u32[]{:S(2)}) %collective-permute-start.19) | collective-permute-done | bytes 524320 | tf_op jit(solution)/shard_map/ppermute | solution.py:185
  186.4 0.6 copy.38
  187.0 1.3 collective-permute-done.20.refs_3_
  188.3 2.4 %shard_map.81 = (bf16[256,512]{1,0:T(8,128)(2,1)S(1)}, bf16[256,512]{1,0:T(8,128)(2,1)S(1)}, bf16[256,512]{1,0:T(8,128)(2,1)S(1)}, bf16[256,512]{1,0:T(8,128)(2,1)S(1)}) custom-call(bf16[256,1024]{1,0:T(8,128)(2,1)S(1)} %get-tuple-element.39.refs_0_, bf16[256,1024]{1,0:T(8,128)(2,1)S(1)} %collective-permute-done.18.refs_1_, ...), custom_call_target="tpu_custom_call" | custom-call | tf_op jit(solution)/shard_map/pallas_call | solution.py:181
  190.9 0.4 collective-permute-start.22
  191.2 1.4 collective-permute-start.23
  192.6 7.4 %collective-permute-done.22.refs_3_ = bf16[256,512]{1,0:T(8,128)(2,1)S(1)} collective-permute-done((bf16[256,512]{1,0:T(8,128)(2,1)S(1)}, bf16[256,512]{1,0:T(8,128)(2,1)S(1)}, u32[]{:S(2)}, u32[]{:S(2)}) %collective-permute-start.22) | collective-permute-done | bytes 262176 | tf_op jit(solution)/shard_map/ppermute | solution.py:185
  200.1 4.4 %collective-permute-done.23.refs_4_ = bf16[256,512]{1,0:T(8,128)(2,1)S(1)} collective-permute-done((bf16[256,512]{1,0:T(8,128)(2,1)S(1)}, bf16[256,512]{1,0:T(8,128)(2,1)S(1)}, u32[]{:S(2)}, u32[]{:S(2)}) %collective-permute-start.23) | collective-permute-done | bytes 262176 | tf_op jit(solution)/shard_map/ppermute | solution.py:185
  204.5 3.4 %shard_map.82 = bf16[256,1024]{1,0:T(8,128)(2,1)S(1)} custom-call(s32[1]{0:T(128)} %bitcast.refs_0_, bf16[256,512]{1,0:T(8,128)(2,1)S(1)} %get-tuple-element.40.refs_1_, bf16[256,512]{1,0:T(8,128)(2,1)S(1)} %collective-permute-done.21.refs_2_, bf16[256,512]{1,0:T(8,128)(2,1)S(1)} %collective-permute-done.22.refs_3_, ...), custom_call_target="tpu_custom_call" | custom-call | tf_op jit(solution)/shard_map/pallas_call | solution.py:161
  208.1 0.5 copy.33
  208.7 17.8 %all_to_all.39 = bf16[1,4,32,2,1024]{4,3,1,0,2:T(2,128)(2,1)S(1)} all-to-all(bf16[1,4,32,2,1024]{4,3,1,0,2:T(2,128)(2,1)S(1)} %copy.33), channel_id=1, replica_groups=mesh['ta'=4,'ha'=4,'wa'=2] {'ha'}, dimensions={2} | all-to-all | bytes 1048576 | tf_op jit(solution)/shard_map/all_to_all | solution.py:241
  226.4 0.5 copy.34
  227.0 1.0 all_to_all.34
  (56 shorter events, 1.5 us)
Async XLA Ops:
  6.5 62.1 %all-gather.6.cloned.1.call-start = ((), (), s32[]{:S(2)}) async-start(), calls=%async_computation.3 | async-start | bytes 2621440 | tf_op jit(solution)/shard_map/all_gather | solution.py:210
  9.1 2.1 copy-start.5
  9.1 111.7 %all-gather.8.cloned.1.call-start = ((), (), s32[]{:S(2)}) async-start(), calls=%async_computation.4 | async-start | bytes 2621440 | tf_op jit(solution)/shard_map/all_gather | solution.py:210
  9.8 153.5 %all-gather.10.cloned.1.call-start = ((), (), s32[]{:S(2)}) async-start(), calls=%async_computation.5 | async-start | bytes 2621440 | tf_op jit(solution)/shard_map/all_gather | solution.py:210
  10.6 5.7 %copy-start.6 = (f32[4,1024]{1,0:T(4,128)S(1)}, f32[4,1024]{1,0:T(4,128)}, u32[]{:S(2)}) copy-start(f32[4,1024]{1,0:T(4,128)} %param.8) | copy-start | bytes 49156
  10.6 182.0 %all-gather.12.cloned.1.call-start = ((), (), s32[]{:S(2)}) async-start(), calls=%async_computation.6 | async-start | bytes 5242880 | tf_op jit(solution)/shard_map/all_gather | solution.py:211
  12.0 13.0 %all-to-all-start = ((bf16[1,4,8,8,1024]{4,3,1,0,2:T(8,128)(2,1)}), bf16[1,4,8,8,1024]{4,3,1,0,2:T(8,128)(2,1)S(1)}, u32[]{:S(2)}, u32[]{:S(2)}) async-start(bf16[1,4,8,8,1024]{4,3,1,0,2:T(8,128)(2,1)} %copy.23), calls=%async_computation | async-start | bytes 1048576 | tf_op jit(solution)/shard_map/all_to_all | solution.py:221
  25.3 19.0 %collective-permute-start.1 = (bf16[256,1024]{1,0:T(8,128)(2,1)S(1)}, bf16[256,1024]{1,0:T(8,128)(2,1)S(1)}, u32[]{:S(2)}, u32[]{:S(2)}) collective-permute-start(bf16[256,1024]{1,0:T(8,128)(2,1)S(1)} %shard_map.73.refs_1_), channel_id=1, source_target_pairs={{0,16},{8,24},{16,0},{24,8},{1,17},{9,25},{17,1},{25,9},{2,18},{10... | collective-permute-start | bytes 1572872 | tf_op jit(solution)/shard_map/ppermute | solution.py:185
  27.0 25.8 %collective-permute-start = (bf16[256,1024]{1,0:T(8,128)(2,1)S(1)}, bf16[256,1024]{1,0:T(8,128)(2,1)}, u32[]{:S(2)}, u32[]{:S(2)}) collective-permute-start(bf16[256,1024]{1,0:T(8,128)(2,1)S(1)} %shard_map.73.refs_1_), channel_id=1, source_target_pairs={{0,8},{8,0},{16,24},{24,16},{1,9},{9,1},{17,25},{25,17},{2,10},{10... | collective-permute-start | bytes 1572872 | tf_op jit(solution)/shard_map/ppermute | solution.py:185
  44.2 8.6 %collective-permute-start.2 = (bf16[256,1024]{1,0:T(8,128)(2,1)S(1)}, bf16[256,1024]{1,0:T(8,128)(2,1)}, u32[]{:S(2)}, u32[]{:S(2)}) collective-permute-start(bf16[256,1024]{1,0:T(8,128)(2,1)S(1)} %collective-permute-done.1.refs_3_), channel_id=1, source_target_pairs={{0,8},{8,0},{16,24},{24,16},{1,9},{9,1},{17,25},{25,17},{2,10},{10... | collective-permute-start | bytes 1572872 | tf_op jit(solution)/shard_map/ppermute | solution.py:185
  50.4 1.7 copy-start.8
  57.7 2.0 collective-permute-start.3
  58.3 8.0 %collective-permute-start.4 = (bf16[256,256]{1,0:T(8,128)(2,1)S(1)}, bf16[256,256]{1,0:T(8,128)(2,1)S(1)}, u32[]{:S(2)}, u32[]{:S(2)}) collective-permute-start(bf16[256,256]{1,0:T(8,128)(2,1)S(1)} %get-tuple-element.27), channel_id=1, source_target_pairs={{0,16},{8,24},{16,0},{24,8},{1,17},{9,25},{17,1},{25,9},{2,18},{10... | collective-permute-start | bytes 393224 | tf_op jit(solution)/shard_map/ppermute | solution.py:185
  58.9 9.7 %collective-permute-start.5 = (bf16[256,256]{1,0:T(8,128)(2,1)S(1)}, bf16[256,256]{1,0:T(8,128)(2,1)S(1)}, u32[]{:S(2)}, u32[]{:S(2)}) collective-permute-start(bf16[256,256]{1,0:T(8,128)(2,1)S(1)} %get-tuple-element.28), channel_id=1, source_target_pairs={{0,24},{8,16},{16,8},{24,0},{1,25},{9,17},{17,9},{25,1},{2,26},{10... | collective-permute-start | bytes 393224 | tf_op jit(solution)/shard_map/ppermute | solution.py:185
  68.6 1.6 copy-start.2
  91.8 18.0 %copy-start.3 = (bf16[1,1024,3,256]{3,1,2,0:T(8,128)(2,1)S(1)}, bf16[1,1024,3,256]{3,1,2,0:T(8,128)(2,1)}, u32[]{:S(2)}) copy-start(bf16[1,1024,3,256]{3,1,2,0:T(8,128)(2,1)} %get-tuple-element.46) | copy-start | bytes 4718596
  92.7 17.1 %collective-permute-start.7 = (bf16[256,1024]{1,0:T(8,128)(2,1)S(1)}, bf16[256,1024]{1,0:T(8,128)(2,1)S(1)}, u32[]{:S(2)}, u32[]{:S(2)}) collective-permute-start(bf16[256,1024]{1,0:T(8,128)(2,1)S(1)} %shard_map.76.refs_1_), channel_id=1, source_target_pairs={{0,16},{8,24},{16,0},{24,8},{1,17},{9,25},{17,1},{25,9},{2,18},{10... | collective-permute-start | bytes 1572872 | tf_op jit(solution)/shard_map/ppermute | solution.py:185
  93.3 20.1 %collective-permute-start.6 = (bf16[256,1024]{1,0:T(8,128)(2,1)S(1)}, bf16[256,1024]{1,0:T(8,128)(2,1)}, u32[]{:S(2)}, u32[]{:S(2)}) collective-permute-start(bf16[256,1024]{1,0:T(8,128)(2,1)S(1)} %shard_map.76.refs_1_), channel_id=1, source_target_pairs={{0,8},{8,0},{16,24},{24,16},{1,9},{9,1},{17,25},{25,17},{2,10},{10... | collective-permute-start | bytes 1572872 | tf_op jit(solution)/shard_map/ppermute | solution.py:185
  109.8 3.6 %collective-permute-start.8 = (bf16[256,1024]{1,0:T(8,128)(2,1)S(1)}, bf16[256,1024]{1,0:T(8,128)(2,1)}, u32[]{:S(2)}, u32[]{:S(2)}) collective-permute-start(bf16[256,1024]{1,0:T(8,128)(2,1)S(1)} %collective-permute-done.7.refs_3_), channel_id=1, source_target_pairs={{0,8},{8,0},{16,24},{24,16},{1,9},{9,1},{17,25},{25,17},{2,10},{10... | collective-permute-start | bytes 1572872 | tf_op jit(solution)/shard_map/ppermute | solution.py:185
  118.6 9.4 %collective-permute-start.10 = (bf16[256,256]{1,0:T(8,128)(2,1)}, bf16[256,256]{1,0:T(8,128)(2,1)S(1)}, u32[]{:S(2)}, u32[]{:S(2)}) collective-permute-start(bf16[256,256]{1,0:T(8,128)(2,1)} %get-tuple-element.31), channel_id=1, source_target_pairs={{0,16},{8,24},{16,0},{24,8},{1,17},{9,25},{17,1},{25,9},{2,18},{10... | collective-permute-start | bytes 393224 | tf_op jit(solution)/shard_map/ppermute | solution.py:185
  119.5 13.7 %collective-permute-start.11 = (bf16[256,256]{1,0:T(8,128)(2,1)S(1)}, bf16[256,256]{1,0:T(8,128)(2,1)S(1)}, u32[]{:S(2)}, u32[]{:S(2)}) collective-permute-start(bf16[256,256]{1,0:T(8,128)(2,1)S(1)} %get-tuple-element.32), channel_id=1, source_target_pairs={{0,24},{8,16},{16,8},{24,0},{1,25},{9,17},{17,9},{25,1},{2,26},{10... | collective-permute-start | bytes 393224 | tf_op jit(solution)/shard_map/ppermute | solution.py:185
  120.5 12.7 %collective-permute-start.9 = (bf16[256,256]{1,0:T(8,128)(2,1)S(1)}, bf16[256,256]{1,0:T(8,128)(2,1)S(1)}, u32[]{:S(2)}, u32[]{:S(2)}) collective-permute-start(bf16[256,256]{1,0:T(8,128)(2,1)S(1)} %get-tuple-element.30), channel_id=1, source_target_pairs={{0,8},{8,0},{16,24},{24,16},{1,9},{9,1},{17,25},{25,17},{2,10},{10... | collective-permute-start | bytes 393224 | tf_op jit(solution)/shard_map/ppermute | solution.py:185
  133.2 1.6 copy-start.1
  136.4 14.5 %collective-permute-start.13 = (bf16[256,1024]{1,0:T(8,128)(2,1)}, bf16[256,1024]{1,0:T(8,128)(2,1)S(1)}, u32[]{:S(2)}, u32[]{:S(2)}) collective-permute-start(bf16[256,1024]{1,0:T(8,128)(2,1)} %get-tuple-element.33.refs_1_), channel_id=1, source_target_pairs={{0,16},{8,24},{16,0},{24,8},{1,17},{9,25},{17,1},{25,9},{2,18},{10... | collective-permute-start | bytes 1572872 | tf_op jit(solution)/shard_map/ppermute | solution.py:185
  137.2 18.5 %collective-permute-start.12 = (bf16[256,1024]{1,0:T(8,128)(2,1)}, bf16[256,1024]{1,0:T(8,128)(2,1)}, u32[]{:S(2)}, u32[]{:S(2)}) collective-permute-start(bf16[256,1024]{1,0:T(8,128)(2,1)} %get-tuple-element.33.refs_1_), channel_id=1, source_target_pairs={{0,8},{8,0},{16,24},{24,16},{1,9},{9,1},{17,25},{25,17},{2,10},{10... | collective-permute-start | bytes 1572872 | tf_op jit(solution)/shard_map/ppermute | solution.py:185
  151.0 4.7 %collective-permute-start.14 = (bf16[256,1024]{1,0:T(8,128)(2,1)S(1)}, bf16[256,1024]{1,0:T(8,128)(2,1)}, u32[]{:S(2)}, u32[]{:S(2)}) collective-permute-start(bf16[256,1024]{1,0:T(8,128)(2,1)S(1)} %collective-permute-done.13.refs_3_), channel_id=1, source_target_pairs={{0,8},{8,0},{16,24},{24,16},{1,9},{9,1},{17,25},{25,17},{2,10},{10... | collective-permute-start | bytes 1572872 | tf_op jit(solution)/shard_map/ppermute | solution.py:185
  153.6 1.9 copy-start.7
  161.5 1.9 collective-permute-start.15
  162.0 6.4 %collective-permute-start.16 = (bf16[256,256]{1,0:T(8,128)(2,1)S(1)}, bf16[256,256]{1,0:T(8,128)(2,1)S(1)}, u32[]{:S(2)}, u32[]{:S(2)}) collective-permute-start(bf16[256,256]{1,0:T(8,128)(2,1)S(1)} %get-tuple-element.36), channel_id=1, source_target_pairs={{0,16},{8,24},{16,0},{24,8},{1,17},{9,25},{17,1},{25,9},{2,18},{10... | collective-permute-start | bytes 393224 | tf_op jit(solution)/shard_map/ppermute | solution.py:185
  162.4 6.9 %collective-permute-start.17 = (bf16[256,256]{1,0:T(8,128)(2,1)S(1)}, bf16[256,256]{1,0:T(8,128)(2,1)S(1)}, u32[]{:S(2)}, u32[]{:S(2)}) collective-permute-start(bf16[256,256]{1,0:T(8,128)(2,1)S(1)} %get-tuple-element.37), channel_id=1, source_target_pairs={{0,24},{8,16},{16,8},{24,0},{1,25},{9,17},{17,9},{25,1},{2,26},{10... | collective-permute-start | bytes 393224 | tf_op jit(solution)/shard_map/ppermute | solution.py:185
  169.3 1.6 copy-start
  170.9 15.5 %copy-start.4 = (bf16[1024,2,512]{2,1,0:T(2,128)(2,1)S(1)}, bf16[1024,2,512]{2,1,0:T(2,128)(2,1)}, u32[]{:S(2)}) copy-start(bf16[1024,2,512]{2,1,0:T(2,128)(2,1)} %param.12) | copy-start | bytes 6291460
  171.7 14.7 %collective-permute-start.19 = (bf16[256,1024]{1,0:T(8,128)(2,1)S(1)}, bf16[256,1024]{1,0:T(8,128)(2,1)S(1)}, u32[]{:S(2)}, u32[]{:S(2)}) collective-permute-start(bf16[256,1024]{1,0:T(8,128)(2,1)S(1)} %get-tuple-element.39.refs_0_), channel_id=1, source_target_pairs={{0,16},{8,24},{16,0},{24,8},{1,17},{9,25},{17,1},{25,9},{2,18},{10... | collective-permute-start | bytes 1572872 | tf_op jit(solution)/shard_map/ppermute | solution.py:185
  172.4 14.6 %collective-permute-start.18 = (bf16[256,1024]{1,0:T(8,128)(2,1)S(1)}, bf16[256,1024]{1,0:T(8,128)(2,1)S(1)}, u32[]{:S(2)}, u32[]{:S(2)}) collective-permute-start(bf16[256,1024]{1,0:T(8,128)(2,1)S(1)} %get-tuple-element.39.refs_0_), channel_id=1, source_target_pairs={{0,8},{8,0},{16,24},{24,16},{1,9},{9,1},{17,25},{25,17},{2,10},{10... | collective-permute-start | bytes 1572872 | tf_op jit(solution)/shard_map/ppermute | solution.py:185
  186.4 1.9 collective-permute-start.20
  190.7 1.9 collective-permute-start.21
  190.9 9.2 %collective-permute-start.22 = (bf16[256,512]{1,0:T(8,128)(2,1)S(1)}, bf16[256,512]{1,0:T(8,128)(2,1)S(1)}, u32[]{:S(2)}, u32[]{:S(2)}) collective-permute-start(bf16[256,512]{1,0:T(8,128)(2,1)S(1)} %get-tuple-element.42), channel_id=1, source_target_pairs={{0,16},{8,24},{16,0},{24,8},{1,17},{9,25},{17,1},{25,9},{2,18},{10... | collective-permute-start | bytes 786440 | tf_op jit(solution)/shard_map/ppermute | solution.py:185
  191.2 13.2 %collective-permute-start.23 = (bf16[256,512]{1,0:T(8,128)(2,1)S(1)}, bf16[256,512]{1,0:T(8,128)(2,1)S(1)}, u32[]{:S(2)}, u32[]{:S(2)}) collective-permute-start(bf16[256,512]{1,0:T(8,128)(2,1)S(1)} %get-tuple-element.43), channel_id=1, source_target_pairs={{0,24},{8,16},{16,8},{24,0},{1,25},{9,17},{17,9},{25,1},{2,26},{10... | collective-permute-start | bytes 786440 | tf_op jit(solution)/shard_map/ppermute | solution.py:185
Sparse Core Ops, SparseCore 0:
  9.2 30.6 all-gather.5
  41.5 25.4 all-gather.7
  68.6 22.5 all-gather.9
  92.6 42.3 all-gather.11
where the time goes:
time: 235 us
  waiting for transfers between devices  112 us (48%)
  blocking collectives  37.8 us (16%)
  local copies, waits for them, and re-layouts  29.2 us (12%)
  Pallas kernels  25.4 us (11%)
  starting transfers between devices  16.4 us (7%)
  between operations  13.4 us (6%)
    ppermute x24, waiting for transfers between devices, flip(): return lax.ppermute(x, 'ta', [(i, i ^ by) for i in range(size)])  102 us
    all_to_all x1, blocking collectives, local(): lax.all_to_all(stream, ('ha', 'wa'), split_axis=0, concat_axis=0, tiled=T...  20.1 us
    all_to_all x1, blocking collectives, local(): return lax.all_to_all(out, 'ha', split_axis=2, concat_axis=3, tiled=True)  17.8 us
    pallas_call x3, Pallas kernels, attention(): call(body, outs, [smem()] + [vmem()] * (count + 2), scratch)  16 us
    unnamed x23, local copies, waits for them, and re-layouts  12.4 us
    ppermute x24, starting transfers between devices, flip(): return lax.ppermute(x, 'ta', [(i, i ^ by) for i in range(size)])  12 us
    all_to_all x1, waiting for transfers between devices, local(): lax.all_to_all(tokens, 'wa', split_axis=2, concat_axis=3, tiled=True)  8.71 us
    pallas_call x4, Pallas kernels, out_product(): call(body, outs, [smem()] + [vmem()] * (count + 3))  6.63 us
  transfers between devices with their start and end apart: 29, of which 14 were waited for; matrix products, arithmetic and copies ran while one was open for 8% of the time, Pallas kernels for 9%

commit v1 on v0

--- a/solution.py
+++ b/solution.py
@@ -138,29 +138,27 @@
     )
 
 
-def out_product(pieces, weight, stream, gain, place, keep):
+def out_product(pieces, weight, stream, gain, keep):
     count = len(pieces)
+    depth = pieces[0].shape[1]
 
     def body(*refs):
-        g_ref = refs[0]
-        x_refs = refs[1 : 1 + count]
-        w_ref, s_ref, gain_ref = refs[1 + count : 4 + count]
+        x_refs = refs[:count]
+        w_ref, s_ref, gain_ref = refs[count : 3 + count]
         total = s_ref[...].astype(F32)
         for r in range(count):
             total = total + jnp.dot(
-                x_refs[r][...], w_ref[g_ref[0] ^ r], preferred_element_type=F32
+                x_refs[r][...], w_ref[:, r].reshape(depth, -1), preferred_element_type=F32
             )
-        refs[4 + count][...] = total.astype(keep)
+        refs[3 + count][...] = total.astype(keep)
         if gain is not None:
-            refs[5 + count][...] = rms(total, gain_ref[...])
+            refs[4 + count][...] = rms(total, gain_ref[...])
 
     outs = [jax.ShapeDtypeStruct(stream.shape, keep)]
     if gain is not None:
         outs.append(jax.ShapeDtypeStruct(stream.shape, BF16))
     spare = jnp.ones((1, stream.shape[1]), F32) if gain is None else gain
-    return call(body, outs, [smem()] + [vmem()] * (count + 3))(
-        place, *pieces, weight, stream, spare
-    )
+    return call(body, outs, [vmem()] * (count + 3))(*pieces, weight, stream, spare)
 
 
 def mlp_hidden(pieces, weight):
@@ -207,8 +205,17 @@
     count = clips * frames * rows * cols
     head_count = qkv_weight.shape[-1] // HEAD_DIM
     gains = jnp.tile(qk_gain, (1, 1, head_count))
-    whole_out = [lax.all_gather(out_weight[p], "ta", axis=0) for p in range(3)]
-    whole_down = lax.all_gather(ffn_out, "ta", axis=0)
+    rank = lax.axis_index("ha")
+
+    def share(weight):
+        part = weight.shape[0] // ha
+        return lax.dynamic_slice_in_dim(weight, rank * part, part, 0)
+
+    def whole(parts):
+        return lax.all_gather(jnp.stack(parts), "ha", axis=0)
+
+    first = whole(spread(share(out_weight[0]), ta))
+    later = jnp.concatenate([share(out_weight[1]), share(out_weight[2]), share(ffn_out)])
     norms = norm_gain[:, None, :]
 
     def attend(normed, p, line, stride, causal):
@@ -222,23 +229,33 @@
     stream = stream.reshape(count, width)
     normed = norm_tokens(stream, norms[0])
     got = attend(normed, 0, cols * wa, 1, False)
-    (stream,) = out_product(got, whole_out[0], stream, None, place, BF16)
+    later, normed = lax.optimization_barrier((later, normed))
+    later = spread(later, ta)
+    step = out_weight.shape[1] // ha
+    second = whole([part[:step] for part in later])
+    third = whole([part[step : 2 * step] for part in later])
+    down = whole([part[2 * step :] for part in later])
+    (stream,) = out_product(got, first, stream, None, BF16)
 
     few = cols // ha
     stream = stream.reshape(frames, rows // wa, wa, ha, few, width)
-    stream = stream.transpose(3, 2, 0, 1, 4, 5).reshape(ha * wa, frames, rows // wa, few, width)
+    stream = stream.transpose(3, 2, 0, 1, 4, 5).reshape(ha * wa, -1, width)
     stream = lax.all_to_all(stream, ("ha", "wa"), split_axis=0, concat_axis=0, tiled=True)
+    stream = stream.reshape(ha * wa, frames, rows // wa, few, width)
     stream = stream.transpose(1, 0, 2, 3, 4).reshape(count, width)
 
     normed = norm_tokens(stream, norms[1])
     got = attend(normed, 1, rows * ha, few, False)
-    stream, normed = out_product(got, whole_out[1], stream, norms[2], place, F32)
+    stream, normed = out_product(got, second, stream, norms[2], F32)
     got = attend(normed, 2, frames * ta, 1, True)
-    stream, normed = out_product(got, whole_out[2], stream, norms[3], place, F32)
+    stream, normed = out_product(got, third, stream, norms[3], F32)
     hidden = exchange(mlp_hidden(spread(normed, ta), ffn_in.reshape(width, -1)))
-    (out,) = out_product(hidden, whole_down, stream, None, place, BF16)
-    out = out.reshape(clips, frames, rows * ha, few, width)
-    return lax.all_to_all(out, "ha", split_axis=2, concat_axis=3, tiled=True)
+    (out,) = out_product(hidden, down, stream, None, BF16)
+    out = out.reshape(frames, ha, rows, few, width).transpose(1, 0, 2, 3, 4)
+    out = out.reshape(ha, -1, width)
+    out = lax.all_to_all(out, "ha", split_axis=0, concat_axis=0, tiled=True)
+    out = out.reshape(ha, frames, rows, few, width).transpose(1, 2, 0, 3, 4)
+    return out.reshape(tokens.shape)
 
 
 def solution(mesh):

time: 235 us -> 279 us (1.19)
  waiting for transfers between devices: 112 us -> 130 us
  blocking collectives: 37.8 us -> 49.1 us
  starting transfers between devices: 16.4 us -> 25.1 us
  other arithmetic: 0 us -> 4.64 us
    all_gather x4, waiting for transfers between devices: 0.01 us -> 35.6 us  [whole(): return lax.all_gather(jnp.stack(parts), 'ha', axis=0)]
    ppermute x24 -> x30, waiting for transfers between devices: 102 us -> 86.4 us  [flip(): return lax.ppermute(x, 'ta', [(i, i ^ by) for i in range(size)])]
    all_to_all x1, blocking collectives: 20.1 us -> 31.9 us  [local(): lax.all_to_all(stream, ('ha', 'wa'), split_axis=0, concat_axis=0, tiled=T...]
    ppermute x24 -> x30, starting transfers between devices: 12 us -> 21.3 us  [flip(): return lax.ppermute(x, 'ta', [(i, i ^ by) for i in range(size)])]
    another operation x0 -> x4, other arithmetic: none -> 4.6 us  [whole(): return lax.all_gather(jnp.stack(parts), 'ha', axis=0)]
    unnamed x23 -> x27, local copies, waits for them, and re-layouts: 12.4 us -> 12.4 us
  transfers between devices with their start and end apart: 29 -> 35, of which waited for: 14 -> 17; matrix products, arithmetic and copies ran while one was open for 8% -> 9% of each run, Pallas kernels for 9% -> 8%
where the time goes in v1:
time: 279 us; the launch traced here: 278 us
  waiting for transfers between devices  130 us (47%)
  blocking collectives  49.1 us (18%)
  local copies, waits for them, and re-layouts  30.1 us (11%)
  Pallas kernels  25.3 us (9%)
  starting transfers between devices  25.1 us (9%)
  between operations  13.6 us (5%)
  other arithmetic  4.64 us (2%)
    ppermute x30, waiting for transfers between devices, flip(): return lax.ppermute(x, 'ta', [(i, i ^ by) for i in range(size)])  86.4 us
    all_gather x4, waiting for transfers between devices, whole(): return lax.all_gather(jnp.stack(parts), 'ha', axis=0)  35.6 us
    all_to_all x1, blocking collectives, local(): lax.all_to_all(stream, ('ha', 'wa'), split_axis=0, concat_axis=0, tiled=T...  31.9 us
    ppermute x30, starting transfers between devices, flip(): return lax.ppermute(x, 'ta', [(i, i ^ by) for i in range(size)])  21.3 us
    all_to_all x1, blocking collectives, local(): out = lax.all_to_all(out, 'ha', split_axis=0, concat_axis=0, tiled=True)  17.2 us
    pallas_call x3, Pallas kernels, attention(): call(body, outs, [smem()] + [vmem()] * (count + 2), scratch)  15.9 us
    unnamed x27, local copies, waits for them, and re-layouts  12.4 us
    all_to_all x1, waiting for transfers between devices, local(): lax.all_to_all(tokens, 'wa', split_axis=2, concat_axis=3, tiled=True)  8.37 us
  transfers between devices with their start and end apart: 35, of which 17 were waited for; matrix products, arithmetic and copies ran while one was open for 9% of the time, Pallas kernels for 8%

profile of v1, /device:TPU:0, one launch (start us, length us, event | category | flops | bytes accessed | tf_op | source)
XLA Modules:
  0.0 278.2 jit_solution(13039842773512007258)
XLA Ops:
  6.5 1.6 fusion.1
  8.1 3.0 %collective-permute-start.7 = (bf16[64,1024]{1,0:T(8,128)(2,1)S(1)}, bf16[64,1024]{1,0:T(8,128)(2,1)S(1)}, u32[]{:S(2)}, u32[]{:S(2)}) collective-permute-start(bf16[64,1024]{1,0:T(8,128)(2,1)S(1)} %fusion.3), channel_id=1, source_target_pairs={{0,16},{8,24},{16,0},{24,8},{1,17},{9,25},{17,1},{25,9},{2,18},{10... | collective-permute-start | bytes 393224 | tf_op jit(solution)/shard_map/ppermute | solution.py:183
  11.2 3.5 %collective-permute-done.7 = bf16[64,1024]{1,0:T(8,128)(2,1)S(1)} collective-permute-done((bf16[64,1024]{1,0:T(8,128)(2,1)S(1)}, bf16[64,1024]{1,0:T(8,128)(2,1)S(1)}, u32[]{:S(2)}, u32[]{:S(2)}) %collective-permute-start.7) | collective-permute-done | bytes 131104 | tf_op jit(solution)/shard_map/ppermute | solution.py:183
  14.7 1.3 collective-permute-done.8
  16.0 0.9 pad_maximum_fusion.1
  16.9 0.8 copy.36
  17.8 3.6 %all-to-all-start = ((bf16[1,4,8,8,1024]{4,3,1,0,2:T(8,128)(2,1)}), bf16[1,4,8,8,1024]{4,3,1,0,2:T(8,128)(2,1)S(1)}, u32[]{:S(2)}, u32[]{:S(2)}) async-start(bf16[1,4,8,8,1024]{4,3,1,0,2:T(8,128)(2,1)} %copy.36), calls=%async_computation | async-start | bytes 1048576 | tf_op jit(solution)/shard_map/all_to_all | solution.py:228
  21.6 8.4 %all-to-all-done = bf16[1,4,8,8,1024]{4,3,1,0,2:T(8,128)(2,1)S(1)} async-done(((bf16[1,4,8,8,1024]{4,3,1,0,2:T(8,128)(2,1)}), bf16[1,4,8,8,1024]{4,3,1,0,2:T(8,128)(2,1)S(1)}, u32[]{:S(2)}, u32[]{:S(2)}) %all-to-all-start) | async-done | bytes 524320 | tf_op jit(solution)/shard_map/all_to_all | solution.py:228
  30.2 1.8 collective-permute-start.16
  32.0 11.4 %collective-permute-done.16 = bf16[256,1024]{1,0:T(8,128)(2,1)S(1)} collective-permute-done((bf16[256,1024]{1,0:T(8,128)(2,1)S(1)}, bf16[256,1024]{1,0:T(8,128)(2,1)S(1)}, u32[]{:S(2)}, u32[]{:S(2)}) %collective-permute-start.16) | collective-permute-done | bytes 524320 | tf_op jit(solution)/shard_map/ppermute | solution.py:183
  43.5 1.8 collective-permute-done.17
  45.4 0.7 slice_bitcast_fusion.4
  46.0 0.9 pad_maximum_fusion.3
  47.0 1.8 pad_maximum_fusion.4
  48.9 1.1 pad_maximum_fusion
  50.0 1.7 collective-permute-start.1
  51.8 12.3 %collective-permute-done.1.refs_3_ = bf16[256,1024]{1,0:T(8,128)(2,1)S(1)} collective-permute-done((bf16[256,1024]{1,0:T(8,128)(2,1)S(1)}, bf16[256,1024]{1,0:T(8,128)(2,1)S(1)}, u32[]{:S(2)}, u32[]{:S(2)}) %collective-permute-start.1) | collective-permute-done | bytes 524320 | tf_op jit(solution)/shard_map/ppermute | solution.py:183
  64.1 4.4 %fusion = (bf16[1,1024,3,256]{3,1,2,0:T(8,128)(2,1)}, bf16[1,1024,3,256]{3,1,2,0:T(8,128)(2,1)}, bf16[1,1024,3,256]{3,1,2,0:T(8,128)(2,1)S(1)}) fusion(bf16[3,1024,3,256]{3,1,2,0:T(8,128)(2,1)} %param.9), kind=kLoop, calls=%fused_computation.25 | loop fusion | bytes 9437184 | tf_op jit(solution)/shard_map/slice | solution.py:222
  68.5 1.8 copy.52
  70.2 1.8 copy.39.refs_5_
  72.0 0.5 slice_bitcast_fusion.12
  72.6 5.0 %shard_map.74 = (bf16[256,256]{1,0:T(8,128)(2,1)S(1)}, bf16[256,256]{1,0:T(8,128)(2,1)S(1)}, bf16[256,256]{1,0:T(8,128)(2,1)S(1)}, bf16[256,256]{1,0:T(8,128)(2,1)S(1)}) custom-call(s32[1]{0:T(128)} %bitcast.refs_0_, bf16[256,1024]{1,0:T(8,128)(2,1)S(1)} %shard_map.73.refs_1_, bf16[256,1024]{1,0:T(8,128)(2,1)} %collective-permute-done.refs_2_, ...), custom_call_target="tpu_custom_call" | custom-call | tf_op jit(solution)/shard_map/pallas_call | solution.py:136
  77.6 0.6 collective-permute-start.3
  78.2 1.7 collective-permute-start.4
  79.9 4.6 %collective-permute-done.4.refs_2_ = bf16[256,256]{1,0:T(8,128)(2,1)S(1)} collective-permute-done((bf16[256,256]{1,0:T(8,128)(2,1)S(1)}, bf16[256,256]{1,0:T(8,128)(2,1)S(1)}, u32[]{:S(2)}, u32[]{:S(2)}) %collective-permute-start.4) | collective-permute-done | bytes 131104 | tf_op jit(solution)/shard_map/ppermute | solution.py:183
  84.5 1.2 collective-permute-done.5.refs_3_
  85.7 1.6 copy-done.4
  87.3 0.7 shard_map.75
  88.2 0.5 copy.57
  89.0 31.9 %all_to_all.25 = bf16[8,32,1024]{2,1,0:T(8,128)(2,1)S(1)} all-to-all(bf16[8,32,1024]{2,1,0:T(8,128)(2,1)S(1)} %reshape.64), channel_id=1, replica_groups=mesh['ta'=4,'ha'=4,'wa'=2] {'ha','wa'}, dimensions={0} | all-to-all | bytes 1048576 | tf_op jit(solution)/shard_map/all_to_all | solution.py:243
  121.2 0.5 copy.42
  122.2 1.6 collective-permute-start.10
  123.7 12.5 %collective-permute-done.10.refs_3_ = bf16[256,1024]{1,0:T(8,128)(2,1)S(1)} collective-permute-done((bf16[256,1024]{1,0:T(8,128)(2,1)S(1)}, bf16[256,1024]{1,0:T(8,128)(2,1)S(1)}, u32[]{:S(2)}, u32[]{:S(2)}) %collective-permute-start.10) | collective-permute-done | bytes 524320 | tf_op jit(solution)/shard_map/ppermute | solution.py:183
  136.3 1.7 copy.53
  138.0 1.7 copy.44.refs_5_
  139.8 5.0 %shard_map.77 = (bf16[256,256]{1,0:T(8,128)(2,1)S(1)}, bf16[256,256]{1,0:T(8,128)(2,1)}, bf16[256,256]{1,0:T(8,128)(2,1)S(1)}, bf16[256,256]{1,0:T(8,128)(2,1)S(1)}) custom-call(s32[1]{0:T(128)} %bitcast.refs_0_, bf16[256,1024]{1,0:T(8,128)(2,1)S(1)} %shard_map.76.refs_1_, bf16[256,1024]{1,0:T(8,128)(2,1)} %collective-permute-done.9.refs_2_, ...), custom_call_target="tpu_custom_call" | custom-call | tf_op jit(solution)/shard_map/pallas_call | solution.py:136
  144.8 0.5 collective-permute-start.12
  145.3 1.5 collective-permute-start.13
  146.8 4.9 %collective-permute-done.13.refs_2_ = bf16[256,256]{1,0:T(8,128)(2,1)S(1)} collective-permute-done((bf16[256,256]{1,0:T(8,128)(2,1)S(1)}, bf16[256,256]{1,0:T(8,128)(2,1)S(1)}, u32[]{:S(2)}, u32[]{:S(2)}) %collective-permute-start.13) | collective-permute-done | bytes 131104 | tf_op jit(solution)/shard_map/ppermute | solution.py:183
  151.7 0.9 collective-permute-done.14.refs_3_
  152.6 1.6 copy-done.2
  154.2 1.6 shard_map.78
  155.9 1.5 collective-permute-start.19
  157.4 0.9 collective-permute-start.18
  158.2 12.5 %collective-permute-done.19.refs_3_ = bf16[256,1024]{1,0:T(8,128)(2,1)S(1)} collective-permute-done((bf16[256,1024]{1,0:T(8,128)(2,1)}, bf16[256,1024]{1,0:T(8,128)(2,1)S(1)}, u32[]{:S(2)}, u32[]{:S(2)}) %collective-permute-start.19) | collective-permute-done | bytes 524320 | tf_op jit(solution)/shard_map/ppermute | solution.py:183
  170.8 2.7 copy.54
  173.5 2.0 copy.46.refs_5_
  175.6 6.0 %shard_map.79 = (bf16[256,256]{1,0:T(8,128)(2,1)S(1)}, bf16[256,256]{1,0:T(8,128)(2,1)}, bf16[256,256]{1,0:T(8,128)(2,1)S(1)}, bf16[256,256]{1,0:T(8,128)(2,1)S(1)}) custom-call(s32[1]{0:T(128)} %bitcast.refs_0_, bf16[256,1024]{1,0:T(8,128)(2,1)} %get-tuple-element.35.refs_1_, bf16[256,1024]{1,0:T(8,128)(2,1)} %collective-permute-done.18.refs_2_, ...), custom_call_target="tpu_custom_call" | custom-call | tf_op jit(solution)/shard_map/pallas_call | solution.py:136
  182.0 1.5 collective-permute-start.22
  183.5 4.9 %collective-permute-done.22.refs_2_ = bf16[256,256]{1,0:T(8,128)(2,1)S(1)} collective-permute-done((bf16[256,256]{1,0:T(8,128)(2,1)S(1)}, bf16[256,256]{1,0:T(8,128)(2,1)S(1)}, u32[]{:S(2)}, u32[]{:S(2)}) %collective-permute-start.22) | collective-permute-done | bytes 131104 | tf_op jit(solution)/shard_map/ppermute | solution.py:183
  188.3 1.1 collective-permute-done.23.refs_3_
  189.4 1.6 copy-done.3
  191.0 0.8 shard_map.80
  191.9 1.6 collective-permute-start.25
  193.5 0.8 collective-permute-start.24
  194.3 12.4 %collective-permute-done.25.refs_2_ = bf16[256,1024]{1,0:T(8,128)(2,1)S(1)} collective-permute-done((bf16[256,1024]{1,0:T(8,128)(2,1)S(1)}, bf16[256,1024]{1,0:T(8,128)(2,1)S(1)}, u32[]{:S(2)}, u32[]{:S(2)}) %collective-permute-start.25) | collective-permute-done | bytes 524320 | tf_op jit(solution)/shard_map/ppermute | solution.py:183
  207.0 0.6 copy.55
  207.5 1.0 collective-permute-done.26.refs_3_
  208.6 2.4 shard_map.81
  211.3 1.5 collective-permute-start.28
  212.9 35.6 %all-gather.15.cloned.1.call-done = bf16[16,128,1024]{2,1,0:T(8,128)(2,1)} async-done(((bf16[4,128,1024]{2,1,0:T(8,128)(2,1)}), bf16[16,128,1024]{2,1,0:T(8,128)(2,1)}) %all-gather.15.cloned.1.call-update) | async-done | bytes 4194320 | tf_op jit(solution)/shard_map/all_gather | solution.py:215
  248.5 3.4 %shard_map.82 = bf16[256,1024]{1,0:T(8,128)(2,1)S(1)} custom-call(bf16[256,512]{1,0:T(8,128)(2,1)S(1)} %get-tuple-element.42.refs_0_, bf16[256,512]{1,0:T(8,128)(2,1)S(1)} %collective-permute-done.27.refs_1_, bf16[256,512]{1,0:T(8,128)(2,1)S(1)} %collective-permute-done.28.refs_2_, bf16[256,512]{1,0:T(8,128)(2,1)S(1)} %collective-permute-done.29.refs_3_, ...), custom_call_target="tpu_custom_call" | custom-call | tf_op jit(solution)/shard_map/pallas_call | solution.py:161
  252.7 17.2 %all_to_all.26 = bf16[4,64,1024]{2,1,0:T(8,128)(2,1)S(1)} all-to-all(bf16[4,64,1024]{2,1,0:T(8,128)(2,1)S(1)} %copy.48), channel_id=1, replica_groups=mesh['ta'=4,'ha'=4,'wa'=2] {'ha'}, dimensions={0} | all-to-all | bytes 1048576 | tf_op jit(solution)/shard_map/all_to_all | solution.py:256
  270.6 1.1 copy.51
  (93 shorter events, 4.9 us)
Async XLA Ops:
  6.5 14.9 %copy-start = (bf16[512,1024]{1,0:T(8,128)(2,1)S(1)}, bf16[512,1024]{1,0:T(8,128)(2,1)}, u32[]{:S(2)}) copy-start(bf16[512,1024]{1,0:T(8,128)(2,1)} %param.13) | copy-start | bytes 3145732
  6.5 79.1 %all-gather.9.cloned.1.call-start = ((), (), s32[]{:S(2)}) async-start(), calls=%async_computation.3 | async-start | bytes 2621440 | tf_op jit(solution)/shard_map/all_gather | solution.py:215
  8.1 8.8 %copy-start.7 = (bf16[1,4,8,8,1024]{4,3,2,1,0:T(8,128)(2,1)S(1)}, bf16[1,4,8,8,1024]{4,3,2,1,0:T(8,128)(2,1)}, u32[]{:S(2)}) copy-start(bf16[1,4,8,8,1024]{4,3,2,1,0:T(8,128)(2,1)} %param.7) | copy-start | bytes 1572868
  8.1 6.5 %collective-permute-start.7 = (bf16[64,1024]{1,0:T(8,128)(2,1)S(1)}, bf16[64,1024]{1,0:T(8,128)(2,1)S(1)}, u32[]{:S(2)}, u32[]{:S(2)}) collective-permute-start(bf16[64,1024]{1,0:T(8,128)(2,1)S(1)} %fusion.3), channel_id=1, source_target_pairs={{0,16},{8,24},{16,0},{24,8},{1,17},{9,25},{17,1},{25,9},{2,18},{10... | collective-permute-start | bytes 393224 | tf_op jit(solution)/shard_map/ppermute | solution.py:183
  11.2 3.5 %collective-permute-start.6 = (bf16[64,1024]{1,0:T(8,128)(2,1)S(1)}, bf16[64,1024]{1,0:T(8,128)(2,1)S(1)}, u32[]{:S(2)}, u32[]{:S(2)}) collective-permute-start(bf16[64,1024]{1,0:T(8,128)(2,1)S(1)} %fusion.3), channel_id=1, source_target_pairs={{0,8},{8,0},{16,24},{24,16},{1,9},{9,1},{17,25},{25,17},{2,10},{10... | collective-permute-start | bytes 393224 | tf_op jit(solution)/shard_map/ppermute | solution.py:183
  14.7 1.3 collective-permute-start.8
  17.8 3.8 %copy-start.8 = (f32[4,1024]{1,0:T(4,128)S(1)}, f32[4,1024]{1,0:T(4,128)}, u32[]{:S(2)}) copy-start(f32[4,1024]{1,0:T(4,128)} %param.8) | copy-start | bytes 49156
  17.8 12.2 %all-to-all-start = ((bf16[1,4,8,8,1024]{4,3,1,0,2:T(8,128)(2,1)}), bf16[1,4,8,8,1024]{4,3,1,0,2:T(8,128)(2,1)S(1)}, u32[]{:S(2)}, u32[]{:S(2)}) async-start(bf16[1,4,8,8,1024]{4,3,1,0,2:T(8,128)(2,1)} %copy.36), calls=%async_computation | async-start | bytes 1048576 | tf_op jit(solution)/shard_map/all_to_all | solution.py:228
  21.4 125.4 %all-gather.11.cloned.1.call-start = ((), (), s32[]{:S(2)}) async-start(), calls=%async_computation.4 | async-start | bytes 2621440 | tf_op jit(solution)/shard_map/all_gather | solution.py:215
  30.2 13.2 %collective-permute-start.16 = (bf16[256,1024]{1,0:T(8,128)(2,1)S(1)}, bf16[256,1024]{1,0:T(8,128)(2,1)S(1)}, u32[]{:S(2)}, u32[]{:S(2)}) collective-permute-start(bf16[256,1024]{1,0:T(8,128)(2,1)S(1)} %pad_maximum_fusion.2), channel_id=1, source_target_pairs={{0,16},{8,24},{16,0},{24,8},{1,17},{9,25},{17,1},{25,9},{2,18},{10... | collective-permute-start | bytes 1572872 | tf_op jit(solution)/shard_map/ppermute | solution.py:183
  32.0 11.5 %collective-permute-start.15 = (bf16[256,1024]{1,0:T(8,128)(2,1)S(1)}, bf16[256,1024]{1,0:T(8,128)(2,1)S(1)}, u32[]{:S(2)}, u32[]{:S(2)}) collective-permute-start(bf16[256,1024]{1,0:T(8,128)(2,1)S(1)} %pad_maximum_fusion.2), channel_id=1, source_target_pairs={{0,8},{8,0},{16,24},{24,16},{1,9},{9,1},{17,25},{25,17},{2,10},{10... | collective-permute-start | bytes 1572872 | tf_op jit(solution)/shard_map/ppermute | solution.py:183
  43.5 1.9 collective-permute-start.17
  46.9 136.5 %all-gather.13.cloned.1.call-start = ((), (), s32[]{:S(2)}) async-start(), calls=%async_computation.5 | async-start | bytes 2621440 | tf_op jit(solution)/shard_map/all_gather | solution.py:215
  48.8 199.7 %all-gather.15.cloned.1.call-start = ((), (), s32[]{:S(2)}) async-start(), calls=%async_computation.6 | async-start | bytes 5242880 | tf_op jit(solution)/shard_map/all_gather | solution.py:215
  50.0 14.0 %collective-permute-start.1 = (bf16[256,1024]{1,0:T(8,128)(2,1)S(1)}, bf16[256,1024]{1,0:T(8,128)(2,1)S(1)}, u32[]{:S(2)}, u32[]{:S(2)}) collective-permute-start(bf16[256,1024]{1,0:T(8,128)(2,1)S(1)} %shard_map.73.refs_1_), channel_id=1, source_target_pairs={{0,16},{8,24},{16,0},{24,8},{1,17},{9,25},{17,1},{25,9},{2,18},{10... | collective-permute-start | bytes 1572872 | tf_op jit(solution)/shard_map/ppermute | solution.py:183
  51.8 20.8 %collective-permute-start = (bf16[256,1024]{1,0:T(8,128)(2,1)S(1)}, bf16[256,1024]{1,0:T(8,128)(2,1)}, u32[]{:S(2)}, u32[]{:S(2)}) collective-permute-start(bf16[256,1024]{1,0:T(8,128)(2,1)S(1)} %shard_map.73.refs_1_), channel_id=1, source_target_pairs={{0,8},{8,0},{16,24},{24,16},{1,9},{9,1},{17,25},{25,17},{2,10},{10... | collective-permute-start | bytes 1572872 | tf_op jit(solution)/shard_map/ppermute | solution.py:183
  64.1 8.6 %collective-permute-start.2 = (bf16[256,1024]{1,0:T(8,128)(2,1)S(1)}, bf16[256,1024]{1,0:T(8,128)(2,1)}, u32[]{:S(2)}, u32[]{:S(2)}) collective-permute-start(bf16[256,1024]{1,0:T(8,128)(2,1)S(1)} %collective-permute-done.1.refs_3_), channel_id=1, source_target_pairs={{0,8},{8,0},{16,24},{24,16},{1,9},{9,1},{17,25},{25,17},{2,10},{10... | collective-permute-start | bytes 1572872 | tf_op jit(solution)/shard_map/ppermute | solution.py:183
  70.2 1.8 copy-start.10
  77.6 2.2 collective-permute-start.3
  78.2 6.3 %collective-permute-start.4 = (bf16[256,256]{1,0:T(8,128)(2,1)S(1)}, bf16[256,256]{1,0:T(8,128)(2,1)S(1)}, u32[]{:S(2)}, u32[]{:S(2)}) collective-permute-start(bf16[256,256]{1,0:T(8,128)(2,1)S(1)} %get-tuple-element.28), channel_id=1, source_target_pairs={{0,16},{8,24},{16,0},{24,8},{1,17},{9,25},{17,1},{25,9},{2,18},{10... | collective-permute-start | bytes 393224 | tf_op jit(solution)/shard_map/ppermute | solution.py:183
  79.9 5.8 %collective-permute-start.5 = (bf16[256,256]{1,0:T(8,128)(2,1)S(1)}, bf16[256,256]{1,0:T(8,128)(2,1)S(1)}, u32[]{:S(2)}, u32[]{:S(2)}) collective-permute-start(bf16[256,256]{1,0:T(8,128)(2,1)S(1)} %get-tuple-element.29), channel_id=1, source_target_pairs={{0,24},{8,16},{16,8},{24,0},{1,25},{9,17},{17,9},{25,1},{2,26},{10... | collective-permute-start | bytes 393224 | tf_op jit(solution)/shard_map/ppermute | solution.py:183
  85.7 1.6 copy-start.4
  121.2 15.1 %copy-start.5 = (bf16[1,1024,3,256]{3,1,2,0:T(8,128)(2,1)S(1)}, bf16[1,1024,3,256]{3,1,2,0:T(8,128)(2,1)}, u32[]{:S(2)}) copy-start(bf16[1,1024,3,256]{3,1,2,0:T(8,128)(2,1)} %get-tuple-element.48) | copy-start | bytes 4718596
  122.2 14.1 %collective-permute-start.10 = (bf16[256,1024]{1,0:T(8,128)(2,1)S(1)}, bf16[256,1024]{1,0:T(8,128)(2,1)S(1)}, u32[]{:S(2)}, u32[]{:S(2)}) collective-permute-start(bf16[256,1024]{1,0:T(8,128)(2,1)S(1)} %shard_map.76.refs_1_), channel_id=1, source_target_pairs={{0,16},{8,24},{16,0},{24,8},{1,17},{9,25},{17,1},{25,9},{2,18},{10... | collective-permute-start | bytes 1572872 | tf_op jit(solution)/shard_map/ppermute | solution.py:183
  123.7 16.1 %collective-permute-start.9 = (bf16[256,1024]{1,0:T(8,128)(2,1)S(1)}, bf16[256,1024]{1,0:T(8,128)(2,1)}, u32[]{:S(2)}, u32[]{:S(2)}) collective-permute-start(bf16[256,1024]{1,0:T(8,128)(2,1)S(1)} %shard_map.76.refs_1_), channel_id=1, source_target_pairs={{0,8},{8,0},{16,24},{24,16},{1,9},{9,1},{17,25},{25,17},{2,10},{10... | collective-permute-start | bytes 1572872 | tf_op jit(solution)/shard_map/ppermute | solution.py:183
  136.3 3.6 %collective-permute-start.11 = (bf16[256,1024]{1,0:T(8,128)(2,1)S(1)}, bf16[256,1024]{1,0:T(8,128)(2,1)}, u32[]{:S(2)}, u32[]{:S(2)}) collective-permute-start(bf16[256,1024]{1,0:T(8,128)(2,1)S(1)} %collective-permute-done.10.refs_3_), channel_id=1, source_target_pairs={{0,8},{8,0},{16,24},{24,16},{1,9},{9,1},{17,25},{25,17},{2,10},{10... | collective-permute-start | bytes 1572872 | tf_op jit(solution)/shard_map/ppermute | solution.py:183
  144.8 2.0 collective-permute-start.12
  145.3 6.4 %collective-permute-start.13 = (bf16[256,256]{1,0:T(8,128)(2,1)S(1)}, bf16[256,256]{1,0:T(8,128)(2,1)S(1)}, u32[]{:S(2)}, u32[]{:S(2)}) collective-permute-start(bf16[256,256]{1,0:T(8,128)(2,1)S(1)} %get-tuple-element.32), channel_id=1, source_target_pairs={{0,16},{8,24},{16,0},{24,8},{1,17},{9,25},{17,1},{25,9},{2,18},{10... | collective-permute-start | bytes 393224 | tf_op jit(solution)/shard_map/ppermute | solution.py:183
  146.8 5.8 %collective-permute-start.14 = (bf16[256,256]{1,0:T(8,128)(2,1)S(1)}, bf16[256,256]{1,0:T(8,128)(2,1)S(1)}, u32[]{:S(2)}, u32[]{:S(2)}) collective-permute-start(bf16[256,256]{1,0:T(8,128)(2,1)S(1)} %get-tuple-element.33), channel_id=1, source_target_pairs={{0,24},{8,16},{16,8},{24,0},{1,25},{9,17},{17,9},{25,1},{2,26},{10... | collective-permute-start | bytes 393224 | tf_op jit(solution)/shard_map/ppermute | solution.py:183
  152.6 1.6 copy-start.2
  155.9 14.8 %collective-permute-start.19 = (bf16[256,1024]{1,0:T(8,128)(2,1)}, bf16[256,1024]{1,0:T(8,128)(2,1)S(1)}, u32[]{:S(2)}, u32[]{:S(2)}) collective-permute-start(bf16[256,1024]{1,0:T(8,128)(2,1)} %get-tuple-element.35.refs_1_), channel_id=1, source_target_pairs={{0,16},{8,24},{16,0},{24,8},{1,17},{9,25},{17,1},{25,9},{2,18},{10... | collective-permute-start | bytes 1572872 | tf_op jit(solution)/shard_map/ppermute | solution.py:183
  157.4 18.2 %collective-permute-start.18 = (bf16[256,1024]{1,0:T(8,128)(2,1)}, bf16[256,1024]{1,0:T(8,128)(2,1)}, u32[]{:S(2)}, u32[]{:S(2)}) collective-permute-start(bf16[256,1024]{1,0:T(8,128)(2,1)} %get-tuple-element.35.refs_1_), channel_id=1, source_target_pairs={{0,8},{8,0},{16,24},{24,16},{1,9},{9,1},{17,25},{25,17},{2,10},{10... | collective-permute-start | bytes 1572872 | tf_op jit(solution)/shard_map/ppermute | solution.py:183
  170.7 4.9 %collective-permute-start.20 = (bf16[256,1024]{1,0:T(8,128)(2,1)S(1)}, bf16[256,1024]{1,0:T(8,128)(2,1)}, u32[]{:S(2)}, u32[]{:S(2)}) collective-permute-start(bf16[256,1024]{1,0:T(8,128)(2,1)S(1)} %collective-permute-done.19.refs_3_), channel_id=1, source_target_pairs={{0,8},{8,0},{16,24},{24,16},{1,9},{9,1},{17,25},{25,17},{2,10},{10... | collective-permute-start | bytes 1572872 | tf_op jit(solution)/shard_map/ppermute | solution.py:183
  173.5 2.0 copy-start.9
  181.6 1.9 collective-permute-start.21
  182.0 6.4 %collective-permute-start.22 = (bf16[256,256]{1,0:T(8,128)(2,1)S(1)}, bf16[256,256]{1,0:T(8,128)(2,1)S(1)}, u32[]{:S(2)}, u32[]{:S(2)}) collective-permute-start(bf16[256,256]{1,0:T(8,128)(2,1)S(1)} %get-tuple-element.38), channel_id=1, source_target_pairs={{0,16},{8,24},{16,0},{24,8},{1,17},{9,25},{17,1},{25,9},{2,18},{10... | collective-permute-start | bytes 393224 | tf_op jit(solution)/shard_map/ppermute | solution.py:183
  183.5 6.0 %collective-permute-start.23 = (bf16[256,256]{1,0:T(8,128)(2,1)S(1)}, bf16[256,256]{1,0:T(8,128)(2,1)S(1)}, u32[]{:S(2)}, u32[]{:S(2)}) collective-permute-start(bf16[256,256]{1,0:T(8,128)(2,1)S(1)} %get-tuple-element.39), channel_id=1, source_target_pairs={{0,24},{8,16},{16,8},{24,0},{1,25},{9,17},{17,9},{25,1},{2,26},{10... | collective-permute-start | bytes 393224 | tf_op jit(solution)/shard_map/ppermute | solution.py:183
  189.4 1.6 copy-start.3
  191.0 15.9 %copy-start.6 = (bf16[1024,2,512]{2,1,0:T(2,128)(2,1)S(1)}, bf16[1024,2,512]{2,1,0:T(2,128)(2,1)}, u32[]{:S(2)}) copy-start(bf16[1024,2,512]{2,1,0:T(2,128)(2,1)} %param.12) | copy-start | bytes 6291460
  191.9 14.8 %collective-permute-start.25 = (bf16[256,1024]{1,0:T(8,128)(2,1)S(1)}, bf16[256,1024]{1,0:T(8,128)(2,1)S(1)}, u32[]{:S(2)}, u32[]{:S(2)}) collective-permute-start(bf16[256,1024]{1,0:T(8,128)(2,1)S(1)} %get-tuple-element.41.refs_0_), channel_id=1, source_target_pairs={{0,16},{8,24},{16,0},{24,8},{1,17},{9,25},{17,1},{25,9},{2,18},{10... | collective-permute-start | bytes 1572872 | tf_op jit(solution)/shard_map/ppermute | solution.py:183
  193.5 14.1 %collective-permute-start.24 = (bf16[256,1024]{1,0:T(8,128)(2,1)S(1)}, bf16[256,1024]{1,0:T(8,128)(2,1)S(1)}, u32[]{:S(2)}, u32[]{:S(2)}) collective-permute-start(bf16[256,1024]{1,0:T(8,128)(2,1)S(1)} %get-tuple-element.41.refs_0_), channel_id=1, source_target_pairs={{0,8},{8,0},{16,24},{24,16},{1,9},{9,1},{17,25},{25,17},{2,10},{10... | collective-permute-start | bytes 1572872 | tf_op jit(solution)/shard_map/ppermute | solution.py:183
  206.6 1.9 collective-permute-start.26
  210.9 37.6 %collective-permute-start.27 = (bf16[256,512]{1,0:T(8,128)(2,1)S(1)}, bf16[256,512]{1,0:T(8,128)(2,1)S(1)}, u32[]{:S(2)}, u32[]{:S(2)}) collective-permute-start(bf16[256,512]{1,0:T(8,128)(2,1)S(1)} %get-tuple-element.43), channel_id=1, source_target_pairs={{0,8},{8,0},{16,24},{24,16},{1,9},{9,1},{17,25},{25,17},{2,10},{10... | collective-permute-start | bytes 786440 | tf_op jit(solution)/shard_map/ppermute | solution.py:183
  211.3 37.2 %collective-permute-start.28 = (bf16[256,512]{1,0:T(8,128)(2,1)S(1)}, bf16[256,512]{1,0:T(8,128)(2,1)S(1)}, u32[]{:S(2)}, u32[]{:S(2)}) collective-permute-start(bf16[256,512]{1,0:T(8,128)(2,1)S(1)} %get-tuple-element.44), channel_id=1, source_target_pairs={{0,16},{8,24},{16,0},{24,8},{1,17},{9,25},{17,1},{25,9},{2,18},{10... | collective-permute-start | bytes 786440 | tf_op jit(solution)/shard_map/ppermute | solution.py:183
  212.9 35.6 %collective-permute-start.29 = (bf16[256,512]{1,0:T(8,128)(2,1)S(1)}, bf16[256,512]{1,0:T(8,128)(2,1)S(1)}, u32[]{:S(2)}, u32[]{:S(2)}) collective-permute-start(bf16[256,512]{1,0:T(8,128)(2,1)S(1)} %get-tuple-element.45), channel_id=1, source_target_pairs={{0,24},{8,16},{16,8},{24,0},{1,25},{9,17},{17,9},{25,1},{2,26},{10... | collective-permute-start | bytes 786440 | tf_op jit(solution)/shard_map/ppermute | solution.py:183
  252.7 19.0 %copy-start.1 = (bf16[512,1024]{1,0:T(8,128)(2,1)S(1)}, bf16[512,1024]{1,0:T(8,128)(2,1)}, u32[]{:S(2)}) copy-start(bf16[512,1024]{1,0:T(8,128)(2,1)} %param.13) | copy-start | bytes 3145732
Sparse Core Ops, SparseCore 0:
  17.0 47.1 all-gather.8
  65.8 55.6 all-gather.10
  123.1 44.3 all-gather.12
  168.9 79.5 all-gather.14

commit v2 on v0

--- a/solution.py
+++ b/solution.py
@@ -237,8 +237,17 @@
     stream, normed = out_product(got, whole_out[2], stream, norms[3], place, F32)
     hidden = exchange(mlp_hidden(spread(normed, ta), ffn_in.reshape(width, -1)))
     (out,) = out_product(hidden, whole_down, stream, None, place, BF16)
-    out = out.reshape(clips, frames, rows * ha, few, width)
-    return lax.all_to_all(out, "ha", split_axis=2, concat_axis=3, tiled=True)
+    out = out.reshape(frames, ha, rows, few, width).transpose(1, 0, 2, 3, 4)
+    out = out.reshape(ha, -1, width)
+    rank = lax.axis_index("ha")
+    whole = jnp.zeros_like(out)
+    for r in range(ha):
+        part = lax.dynamic_slice_in_dim(out, rank ^ r, 1, 0)
+        if r:
+            part = lax.ppermute(part, "ha", [(i, i ^ r) for i in range(ha)])
+        whole = lax.dynamic_update_slice_in_dim(whole, part, rank ^ r, 0)
+    whole = whole.reshape(ha, frames, rows, few, width).transpose(1, 2, 0, 3, 4)
+    return whole.reshape(tokens.shape)
 
 
 def solution(mesh):

time: 235 us -> 244 us (1.038)
  blocking collectives: 37.8 us -> 20.1 us
  waiting for transfers between devices: 112 us -> 126 us
  local copies, waits for them, and re-layouts: 29.2 us -> 37.1 us
  starting transfers between devices: 16.4 us -> 21 us
    all_to_all x1 -> x0, blocking collectives: 17.8 us -> none  [local(): return lax.all_to_all(out, 'ha', split_axis=2, concat_axis=3, tiled=True)]
    ppermute x0 -> x3, waiting for transfers between devices: none -> 13.4 us  [local(): part = lax.ppermute(part, 'ha', [(i, i ^ r) for i in range(ha)])]
    dynamic_update_slice x0 -> x4, local copies, waits for them, and re-layouts: none -> 6.91 us  [local(): whole = lax.dynamic_update_slice_in_dim(whole, part, rank ^ r, 0)]
    ppermute x0 -> x3, starting transfers between devices: none -> 4.44 us  [local(): part = lax.ppermute(part, 'ha', [(i, i ^ r) for i in range(ha)])]
  transfers between devices with their start and end apart: 29 -> 32, of which waited for: 14 -> 16; matrix products, arithmetic and copies ran while one was open for 8% -> 10% of each run, Pallas kernels for 9% -> 9%
where the time goes in v2:
time: 244 us; the launch traced here: 243 us
  waiting for transfers between devices  126 us (52%)
  local copies, waits for them, and re-layouts  37.1 us (15%)
  Pallas kernels  25.4 us (10%)
  starting transfers between devices  21 us (9%)
  blocking collectives  20.1 us (8%)
  between operations  13.4 us (5%)
    ppermute x24, waiting for transfers between devices, flip(): return lax.ppermute(x, 'ta', [(i, i ^ by) for i in range(size)])  101 us
    all_to_all x1, blocking collectives, local(): lax.all_to_all(stream, ('ha', 'wa'), split_axis=0, concat_axis=0, tiled=T...  20.1 us
    pallas_call x3, Pallas kernels, attention(): call(body, outs, [smem()] + [vmem()] * (count + 2), scratch)  16 us
    ppermute x3, waiting for transfers between devices, local(): part = lax.ppermute(part, 'ha', [(i, i ^ r) for i in range(ha)])  13.4 us
    unnamed x23, local copies, waits for them, and re-layouts  12.4 us
    ppermute x24, starting transfers between devices, flip(): return lax.ppermute(x, 'ta', [(i, i ^ by) for i in range(size)])  12.2 us
    all_to_all x1, waiting for transfers between devices, local(): lax.all_to_all(tokens, 'wa', split_axis=2, concat_axis=3, tiled=True)  8.71 us
    dynamic_update_slice x4, local copies, waits for them, and re-layouts, local(): whole = lax.dynamic_update_slice_in_dim(whole, part, rank ^ r, 0)  6.91 us
  transfers between devices with their start and end apart: 32, of which 16 were waited for; matrix products, arithmetic and copies ran while one was open for 10% of the time, Pallas kernels for 9%

profile of v2, /device:TPU:0, one launch (start us, length us, event | category | flops | bytes accessed | tf_op | source)
XLA Modules:
  0.0 242.6 jit_solution(2623928795364522423)
XLA Ops:
  6.5 2.6 %fusion.1 = (bf16[1,256,1024]{2,1,0:T(8,128)(2,1)}, bf16[1,256,1024]{2,1,0:T(8,128)(2,1)}, bf16[1,256,1024]{2,1,0:T(8,128)(2,1)}) fusion(bf16[3,256,1024]{2,1,0:T(8,128)(2,1)} %param.11), kind=kLoop, calls=%fused_computation.8 | loop fusion | bytes 3145728 | tf_op jit(solution)/shard_map/slice | solution.py:210
  9.2 0.7 all-gather.8.cloned.1.call-update
  9.9 0.7 all-gather.10.cloned.1.call-update
  10.7 0.5 all-gather.12.cloned.1.call-update
  11.2 0.8 copy.33
  12.0 4.3 %all-to-all-start = ((bf16[1,4,8,8,1024]{4,3,1,0,2:T(8,128)(2,1)}), bf16[1,4,8,8,1024]{4,3,1,0,2:T(8,128)(2,1)S(1)}, u32[]{:S(2)}, u32[]{:S(2)}) async-start(bf16[1,4,8,8,1024]{4,3,1,0,2:T(8,128)(2,1)} %copy.33), calls=%async_computation | async-start | bytes 1048576 | tf_op jit(solution)/shard_map/all_to_all | solution.py:221
  16.3 8.7 %all-to-all-done = bf16[1,4,8,8,1024]{4,3,1,0,2:T(8,128)(2,1)S(1)} async-done(((bf16[1,4,8,8,1024]{4,3,1,0,2:T(8,128)(2,1)}), bf16[1,4,8,8,1024]{4,3,1,0,2:T(8,128)(2,1)S(1)}, u32[]{:S(2)}, u32[]{:S(2)}) %all-to-all-start) | async-done | bytes 524320 | tf_op jit(solution)/shard_map/all_to_all | solution.py:221
  25.3 1.8 collective-permute-start.1
  27.1 17.2 %collective-permute-done.1.refs_3_ = bf16[256,1024]{1,0:T(8,128)(2,1)S(1)} collective-permute-done((bf16[256,1024]{1,0:T(8,128)(2,1)S(1)}, bf16[256,1024]{1,0:T(8,128)(2,1)S(1)}, u32[]{:S(2)}, u32[]{:S(2)}) %collective-permute-start.1) | collective-permute-done | bytes 524320 | tf_op jit(solution)/shard_map/ppermute | solution.py:185
  44.3 4.4 %fusion = (bf16[1,1024,3,256]{3,1,2,0:T(8,128)(2,1)}, bf16[1,1024,3,256]{3,1,2,0:T(8,128)(2,1)}, bf16[1,1024,3,256]{3,1,2,0:T(8,128)(2,1)S(1)}) fusion(bf16[3,1024,3,256]{3,1,2,0:T(8,128)(2,1)} %param.9), kind=kLoop, calls=%fused_computation.7 | loop fusion | bytes 9437184 | tf_op jit(solution)/shard_map/slice | solution.py:215
  48.7 1.7 copy.46
  50.4 1.7 copy.36.refs_5_
  52.1 0.6 slice_bitcast_fusion
  52.8 4.9 %shard_map.74 = (bf16[256,256]{1,0:T(8,128)(2,1)S(1)}, bf16[256,256]{1,0:T(8,128)(2,1)S(1)}, bf16[256,256]{1,0:T(8,128)(2,1)S(1)}, bf16[256,256]{1,0:T(8,128)(2,1)S(1)}) custom-call(s32[1]{0:T(128)} %bitcast.refs_0_, bf16[256,1024]{1,0:T(8,128)(2,1)S(1)} %shard_map.73.refs_1_, bf16[256,1024]{1,0:T(8,128)(2,1)} %collective-permute-done.refs_2_, ...), custom_call_target="tpu_custom_call" | custom-call | tf_op jit(solution)/shard_map/pallas_call | solution.py:136
  57.7 0.6 collective-permute-start.3
  58.3 0.6 collective-permute-start.4
  58.8 0.9 collective-permute-start.5
  59.7 6.6 %collective-permute-done.4.refs_3_ = bf16[256,256]{1,0:T(8,128)(2,1)S(1)} collective-permute-done((bf16[256,256]{1,0:T(8,128)(2,1)S(1)}, bf16[256,256]{1,0:T(8,128)(2,1)S(1)}, u32[]{:S(2)}, u32[]{:S(2)}) %collective-permute-start.4) | collective-permute-done | bytes 131104 | tf_op jit(solution)/shard_map/ppermute | solution.py:185
  66.4 2.3 collective-permute-done.5.refs_4_
  68.7 1.6 copy-done.2
  70.3 0.7 shard_map.75
  71.2 0.5 copy.37
  71.7 20.1 %all_to_all.20 = bf16[8,4,4,2,1024]{4,3,2,1,0:T(2,128)(2,1)S(1)} all-to-all(bf16[8,4,4,2,1024]{4,3,2,1,0:T(2,128)(2,1)S(1)} %bitcast.39), channel_id=1, replica_groups=mesh['ta'=4,'ha'=4,'wa'=2] {'ha','wa'}, dimensions={0} | all-to-all | bytes 1048576 | tf_op jit(solution)/shard_map/all_to_all | solution.py:230
  91.8 0.5 copy.38
  92.7 0.6 collective-permute-start.7
  93.3 16.4 %collective-permute-done.7.refs_3_ = bf16[256,1024]{1,0:T(8,128)(2,1)S(1)} collective-permute-done((bf16[256,1024]{1,0:T(8,128)(2,1)S(1)}, bf16[256,1024]{1,0:T(8,128)(2,1)S(1)}, u32[]{:S(2)}, u32[]{:S(2)}) %collective-permute-start.7) | collective-permute-done | bytes 524320 | tf_op jit(solution)/shard_map/ppermute | solution.py:185
  109.7 1.8 copy.47
  111.5 1.7 copy.40.refs_5_
  113.3 5.3 %shard_map.77 = (bf16[256,256]{1,0:T(8,128)(2,1)S(1)}, bf16[256,256]{1,0:T(8,128)(2,1)S(1)}, bf16[256,256]{1,0:T(8,128)(2,1)}, bf16[256,256]{1,0:T(8,128)(2,1)S(1)}) custom-call(s32[1]{0:T(128)} %bitcast.refs_0_, bf16[256,1024]{1,0:T(8,128)(2,1)S(1)} %shard_map.76.refs_1_, bf16[256,1024]{1,0:T(8,128)(2,1)} %collective-permute-done.6.refs_2_, ...), custom_call_target="tpu_custom_call" | custom-call | tf_op jit(solution)/shard_map/pallas_call | solution.py:136
  118.6 0.8 collective-permute-start.10
  119.5 1.0 collective-permute-start.11
  120.8 7.2 %collective-permute-done.10.refs_3_ = bf16[256,256]{1,0:T(8,128)(2,1)S(1)} collective-permute-done((bf16[256,256]{1,0:T(8,128)(2,1)}, bf16[256,256]{1,0:T(8,128)(2,1)S(1)}, u32[]{:S(2)}, u32[]{:S(2)}) %collective-permute-start.10) | collective-permute-done | bytes 131104 | tf_op jit(solution)/shard_map/ppermute | solution.py:185
  128.0 5.1 %collective-permute-done.11.refs_4_ = bf16[256,256]{1,0:T(8,128)(2,1)S(1)} collective-permute-done((bf16[256,256]{1,0:T(8,128)(2,1)S(1)}, bf16[256,256]{1,0:T(8,128)(2,1)S(1)}, u32[]{:S(2)}, u32[]{:S(2)}) %collective-permute-start.11) | collective-permute-done | bytes 131104 | tf_op jit(solution)/shard_map/ppermute | solution.py:185
  133.1 1.6 copy-done.1
  134.7 1.6 shard_map.78
  136.4 0.8 collective-permute-start.13
  137.2 13.8 %collective-permute-done.13.refs_3_ = bf16[256,1024]{1,0:T(8,128)(2,1)S(1)} collective-permute-done((bf16[256,1024]{1,0:T(8,128)(2,1)}, bf16[256,1024]{1,0:T(8,128)(2,1)S(1)}, u32[]{:S(2)}, u32[]{:S(2)}) %collective-permute-start.13) | collective-permute-done | bytes 524320 | tf_op jit(solution)/shard_map/ppermute | solution.py:185
  151.0 2.6 %copy.48 = bf16[1,1024,3,256]{1,3,2,0:T(8,128)(2,1)} copy(bf16[1,1024,3,256]{3,1,2,0:T(8,128)(2,1)} %get-tuple-element.45) | data formatting | bytes 3145728
  153.6 1.9 copy.42.refs_5_
  155.7 5.9 %shard_map.79 = (bf16[256,256]{1,0:T(8,128)(2,1)S(1)}, bf16[256,256]{1,0:T(8,128)(2,1)}, bf16[256,256]{1,0:T(8,128)(2,1)S(1)}, bf16[256,256]{1,0:T(8,128)(2,1)S(1)}) custom-call(s32[1]{0:T(128)} %bitcast.refs_0_, bf16[256,1024]{1,0:T(8,128)(2,1)} %get-tuple-element.33.refs_1_, bf16[256,1024]{1,0:T(8,128)(2,1)} %collective-permute-done.12.refs_2_, ...), custom_call_target="tpu_custom_call" | custom-call | tf_op jit(solution)/shard_map/pallas_call | solution.py:136
  161.5 0.5 collective-permute-start.15
  162.4 0.9 collective-permute-start.17
  163.4 5.0 %collective-permute-done.16.refs_3_ = bf16[256,256]{1,0:T(8,128)(2,1)S(1)} collective-permute-done((bf16[256,256]{1,0:T(8,128)(2,1)S(1)}, bf16[256,256]{1,0:T(8,128)(2,1)S(1)}, u32[]{:S(2)}, u32[]{:S(2)}) %collective-permute-start.16) | collective-permute-done | bytes 131104 | tf_op jit(solution)/shard_map/ppermute | solution.py:185
  168.4 0.9 collective-permute-done.17.refs_4_
  169.3 1.6 copy-done
  170.9 0.8 shard_map.80
  171.7 0.6 collective-permute-start.19
  172.7 13.7 %collective-permute-done.19.refs_2_ = bf16[256,1024]{1,0:T(8,128)(2,1)S(1)} collective-permute-done((bf16[256,1024]{1,0:T(8,128)(2,1)S(1)}, bf16[256,1024]{1,0:T(8,128)(2,1)S(1)}, u32[]{:S(2)}, u32[]{:S(2)}) %collective-permute-start.19) | collective-permute-done | bytes 524320 | tf_op jit(solution)/shard_map/ppermute | solution.py:185
  186.4 0.6 copy.49
  187.0 1.3 collective-permute-done.20.refs_3_
  188.3 2.4 shard_map.81
  191.3 1.3 collective-permute-start.23
  192.6 7.4 %collective-permute-done.22.refs_3_ = bf16[256,512]{1,0:T(8,128)(2,1)S(1)} collective-permute-done((bf16[256,512]{1,0:T(8,128)(2,1)S(1)}, bf16[256,512]{1,0:T(8,128)(2,1)S(1)}, u32[]{:S(2)}, u32[]{:S(2)}) %collective-permute-start.22) | collective-permute-done | bytes 262176 | tf_op jit(solution)/shard_map/ppermute | solution.py:185
  200.1 4.4 %collective-permute-done.23.refs_4_ = bf16[256,512]{1,0:T(8,128)(2,1)S(1)} collective-permute-done((bf16[256,512]{1,0:T(8,128)(2,1)S(1)}, bf16[256,512]{1,0:T(8,128)(2,1)S(1)}, u32[]{:S(2)}, u32[]{:S(2)}) %collective-permute-start.23) | collective-permute-done | bytes 262176 | tf_op jit(solution)/shard_map/ppermute | solution.py:185
  204.5 3.4 %shard_map.82 = bf16[256,1024]{1,0:T(8,128)(2,1)S(1)} custom-call(s32[1]{0:T(128)} %bitcast.refs_0_, bf16[256,512]{1,0:T(8,128)(2,1)S(1)} %get-tuple-element.40.refs_1_, bf16[256,512]{1,0:T(8,128)(2,1)S(1)} %collective-permute-done.21.refs_2_, bf16[256,512]{1,0:T(8,128)(2,1)S(1)} %collective-permute-done.22.refs_3_, ...), custom_call_target="tpu_custom_call" | custom-call | tf_op jit(solution)/shard_map/pallas_call | solution.py:161
  208.5 1.1 constant_dynamic-slice_fusion
  209.8 4.3 %collective-permute-start.26 = (bf16[1,64,1024]{2,0,1:T(2,128)(2,1)S(1)}, bf16[1,64,1024]{2,0,1:T(2,128)(2,1)S(1)}, u32[]{:S(2)}, u32[]{:S(2)}) collective-permute-start(bf16[1,64,1024]{2,0,1:T(2,128)(2,1)S(1)} %get-tuple-element.51), channel_id=1, source_target_pairs={{0,6},{2,4},{4,2},{6,0},{1,7},{3,5},{5,3},{7,1},{8,14},{10,12},{12... | collective-permute-start | bytes 393224 | tf_op jit(solution)/shard_map/ppermute | solution.py:247
  214.2 1.7 dynamic_update_slice.12
  216.0 6.3 %collective-permute-done.24 = bf16[1,64,1024]{2,0,1:T(2,128)(2,1)S(1)} collective-permute-done((bf16[1,64,1024]{2,0,1:T(2,128)(2,1)S(1)}, bf16[1,64,1024]{2,0,1:T(2,128)(2,1)S(1)}, u32[]{:S(2)}, u32[]{:S(2)}) %collective-permute-start.24) | collective-permute-done | bytes 131104 | tf_op jit(solution)/shard_map/ppermute | solution.py:247
  222.3 1.7 dynamic_update_slice.13
  224.0 7.1 %collective-permute-done.25 = bf16[1,64,1024]{2,0,1:T(2,128)(2,1)S(1)} collective-permute-done((bf16[1,64,1024]{2,0,1:T(2,128)(2,1)S(1)}, bf16[1,64,1024]{2,0,1:T(2,128)(2,1)S(1)}, u32[]{:S(2)}, u32[]{:S(2)}) %collective-permute-start.25) | collective-permute-done | bytes 131104 | tf_op jit(solution)/shard_map/ppermute | solution.py:247
  231.2 1.7 dynamic_update_slice.14
  232.9 1.7 dynamic_update_slice.15
  234.9 1.1 copy.45
  (67 shorter events, 4.2 us)
Async XLA Ops:
  6.5 62.1 %all-gather.6.cloned.1.call-start = ((), (), s32[]{:S(2)}) async-start(), calls=%async_computation.2 | async-start | bytes 2621440 | tf_op jit(solution)/shard_map/all_gather | solution.py:210
  9.1 2.1 copy-start.5
  9.1 111.6 %all-gather.8.cloned.1.call-start = ((), (), s32[]{:S(2)}) async-start(), calls=%async_computation.3 | async-start | bytes 2621440 | tf_op jit(solution)/shard_map/all_gather | solution.py:210
  9.9 153.5 %all-gather.10.cloned.1.call-start = ((), (), s32[]{:S(2)}) async-start(), calls=%async_computation.4 | async-start | bytes 2621440 | tf_op jit(solution)/shard_map/all_gather | solution.py:210
  10.6 5.7 %copy-start.6 = (f32[4,1024]{1,0:T(4,128)S(1)}, f32[4,1024]{1,0:T(4,128)}, u32[]{:S(2)}) copy-start(f32[4,1024]{1,0:T(4,128)} %param.8) | copy-start | bytes 49156
  10.6 182.0 %all-gather.12.cloned.1.call-start = ((), (), s32[]{:S(2)}) async-start(), calls=%async_computation.5 | async-start | bytes 5242880 | tf_op jit(solution)/shard_map/all_gather | solution.py:211
  12.0 13.0 %all-to-all-start = ((bf16[1,4,8,8,1024]{4,3,1,0,2:T(8,128)(2,1)}), bf16[1,4,8,8,1024]{4,3,1,0,2:T(8,128)(2,1)S(1)}, u32[]{:S(2)}, u32[]{:S(2)}) async-start(bf16[1,4,8,8,1024]{4,3,1,0,2:T(8,128)(2,1)} %copy.33), calls=%async_computation | async-start | bytes 1048576 | tf_op jit(solution)/shard_map/all_to_all | solution.py:221
  25.3 19.0 %collective-permute-start.1 = (bf16[256,1024]{1,0:T(8,128)(2,1)S(1)}, bf16[256,1024]{1,0:T(8,128)(2,1)S(1)}, u32[]{:S(2)}, u32[]{:S(2)}) collective-permute-start(bf16[256,1024]{1,0:T(8,128)(2,1)S(1)} %shard_map.73.refs_1_), channel_id=1, source_target_pairs={{0,16},{8,24},{16,0},{24,8},{1,17},{9,25},{17,1},{25,9},{2,18},{10... | collective-permute-start | bytes 1572872 | tf_op jit(solution)/shard_map/ppermute | solution.py:185
  27.1 25.7 %collective-permute-start = (bf16[256,1024]{1,0:T(8,128)(2,1)S(1)}, bf16[256,1024]{1,0:T(8,128)(2,1)}, u32[]{:S(2)}, u32[]{:S(2)}) collective-permute-start(bf16[256,1024]{1,0:T(8,128)(2,1)S(1)} %shard_map.73.refs_1_), channel_id=1, source_target_pairs={{0,8},{8,0},{16,24},{24,16},{1,9},{9,1},{17,25},{25,17},{2,10},{10... | collective-permute-start | bytes 1572872 | tf_op jit(solution)/shard_map/ppermute | solution.py:185
  44.3 8.5 %collective-permute-start.2 = (bf16[256,1024]{1,0:T(8,128)(2,1)S(1)}, bf16[256,1024]{1,0:T(8,128)(2,1)}, u32[]{:S(2)}, u32[]{:S(2)}) collective-permute-start(bf16[256,1024]{1,0:T(8,128)(2,1)S(1)} %collective-permute-done.1.refs_3_), channel_id=1, source_target_pairs={{0,8},{8,0},{16,24},{24,16},{1,9},{9,1},{17,25},{25,17},{2,10},{10... | collective-permute-start | bytes 1572872 | tf_op jit(solution)/shard_map/ppermute | solution.py:185
  50.4 1.7 copy-start.8
  57.7 2.0 collective-permute-start.3
  58.3 8.1 %collective-permute-start.4 = (bf16[256,256]{1,0:T(8,128)(2,1)S(1)}, bf16[256,256]{1,0:T(8,128)(2,1)S(1)}, u32[]{:S(2)}, u32[]{:S(2)}) collective-permute-start(bf16[256,256]{1,0:T(8,128)(2,1)S(1)} %get-tuple-element.27), channel_id=1, source_target_pairs={{0,16},{8,24},{16,0},{24,8},{1,17},{9,25},{17,1},{25,9},{2,18},{10... | collective-permute-start | bytes 393224 | tf_op jit(solution)/shard_map/ppermute | solution.py:185
  58.8 9.8 %collective-permute-start.5 = (bf16[256,256]{1,0:T(8,128)(2,1)S(1)}, bf16[256,256]{1,0:T(8,128)(2,1)S(1)}, u32[]{:S(2)}, u32[]{:S(2)}) collective-permute-start(bf16[256,256]{1,0:T(8,128)(2,1)S(1)} %get-tuple-element.28), channel_id=1, source_target_pairs={{0,24},{8,16},{16,8},{24,0},{1,25},{9,17},{17,9},{25,1},{2,26},{10... | collective-permute-start | bytes 393224 | tf_op jit(solution)/shard_map/ppermute | solution.py:185
  68.7 1.6 copy-start.2
  91.8 17.9 %copy-start.3 = (bf16[1,1024,3,256]{3,1,2,0:T(8,128)(2,1)S(1)}, bf16[1,1024,3,256]{3,1,2,0:T(8,128)(2,1)}, u32[]{:S(2)}) copy-start(bf16[1,1024,3,256]{3,1,2,0:T(8,128)(2,1)} %get-tuple-element.46) | copy-start | bytes 4718596
  92.7 17.0 %collective-permute-start.7 = (bf16[256,1024]{1,0:T(8,128)(2,1)S(1)}, bf16[256,1024]{1,0:T(8,128)(2,1)S(1)}, u32[]{:S(2)}, u32[]{:S(2)}) collective-permute-start(bf16[256,1024]{1,0:T(8,128)(2,1)S(1)} %shard_map.76.refs_1_), channel_id=1, source_target_pairs={{0,16},{8,24},{16,0},{24,8},{1,17},{9,25},{17,1},{25,9},{2,18},{10... | collective-permute-start | bytes 1572872 | tf_op jit(solution)/shard_map/ppermute | solution.py:185
  93.3 20.0 %collective-permute-start.6 = (bf16[256,1024]{1,0:T(8,128)(2,1)S(1)}, bf16[256,1024]{1,0:T(8,128)(2,1)}, u32[]{:S(2)}, u32[]{:S(2)}) collective-permute-start(bf16[256,1024]{1,0:T(8,128)(2,1)S(1)} %shard_map.76.refs_1_), channel_id=1, source_target_pairs={{0,8},{8,0},{16,24},{24,16},{1,9},{9,1},{17,25},{25,17},{2,10},{10... | collective-permute-start | bytes 1572872 | tf_op jit(solution)/shard_map/ppermute | solution.py:185
  109.7 3.6 %collective-permute-start.8 = (bf16[256,1024]{1,0:T(8,128)(2,1)S(1)}, bf16[256,1024]{1,0:T(8,128)(2,1)}, u32[]{:S(2)}, u32[]{:S(2)}) collective-permute-start(bf16[256,1024]{1,0:T(8,128)(2,1)S(1)} %collective-permute-done.7.refs_3_), channel_id=1, source_target_pairs={{0,8},{8,0},{16,24},{24,16},{1,9},{9,1},{17,25},{25,17},{2,10},{10... | collective-permute-start | bytes 1572872 | tf_op jit(solution)/shard_map/ppermute | solution.py:185
  118.6 9.4 %collective-permute-start.10 = (bf16[256,256]{1,0:T(8,128)(2,1)}, bf16[256,256]{1,0:T(8,128)(2,1)S(1)}, u32[]{:S(2)}, u32[]{:S(2)}) collective-permute-start(bf16[256,256]{1,0:T(8,128)(2,1)} %get-tuple-element.31), channel_id=1, source_target_pairs={{0,16},{8,24},{16,0},{24,8},{1,17},{9,25},{17,1},{25,9},{2,18},{10... | collective-permute-start | bytes 393224 | tf_op jit(solution)/shard_map/ppermute | solution.py:185
  119.5 13.7 %collective-permute-start.11 = (bf16[256,256]{1,0:T(8,128)(2,1)S(1)}, bf16[256,256]{1,0:T(8,128)(2,1)S(1)}, u32[]{:S(2)}, u32[]{:S(2)}) collective-permute-start(bf16[256,256]{1,0:T(8,128)(2,1)S(1)} %get-tuple-element.32), channel_id=1, source_target_pairs={{0,24},{8,16},{16,8},{24,0},{1,25},{9,17},{17,9},{25,1},{2,26},{10... | collective-permute-start | bytes 393224 | tf_op jit(solution)/shard_map/ppermute | solution.py:185
  120.4 12.7 %collective-permute-start.9 = (bf16[256,256]{1,0:T(8,128)(2,1)S(1)}, bf16[256,256]{1,0:T(8,128)(2,1)S(1)}, u32[]{:S(2)}, u32[]{:S(2)}) collective-permute-start(bf16[256,256]{1,0:T(8,128)(2,1)S(1)} %get-tuple-element.30), channel_id=1, source_target_pairs={{0,8},{8,0},{16,24},{24,16},{1,9},{9,1},{17,25},{25,17},{2,10},{10... | collective-permute-start | bytes 393224 | tf_op jit(solution)/shard_map/ppermute | solution.py:185
  133.1 1.6 copy-start.1
  136.4 14.6 %collective-permute-start.13 = (bf16[256,1024]{1,0:T(8,128)(2,1)}, bf16[256,1024]{1,0:T(8,128)(2,1)S(1)}, u32[]{:S(2)}, u32[]{:S(2)}) collective-permute-start(bf16[256,1024]{1,0:T(8,128)(2,1)} %get-tuple-element.33.refs_1_), channel_id=1, source_target_pairs={{0,16},{8,24},{16,0},{24,8},{1,17},{9,25},{17,1},{25,9},{2,18},{10... | collective-permute-start | bytes 1572872 | tf_op jit(solution)/shard_map/ppermute | solution.py:185
  137.2 18.5 %collective-permute-start.12 = (bf16[256,1024]{1,0:T(8,128)(2,1)}, bf16[256,1024]{1,0:T(8,128)(2,1)}, u32[]{:S(2)}, u32[]{:S(2)}) collective-permute-start(bf16[256,1024]{1,0:T(8,128)(2,1)} %get-tuple-element.33.refs_1_), channel_id=1, source_target_pairs={{0,8},{8,0},{16,24},{24,16},{1,9},{9,1},{17,25},{25,17},{2,10},{10... | collective-permute-start | bytes 1572872 | tf_op jit(solution)/shard_map/ppermute | solution.py:185
  151.0 4.7 %collective-permute-start.14 = (bf16[256,1024]{1,0:T(8,128)(2,1)S(1)}, bf16[256,1024]{1,0:T(8,128)(2,1)}, u32[]{:S(2)}, u32[]{:S(2)}) collective-permute-start(bf16[256,1024]{1,0:T(8,128)(2,1)S(1)} %collective-permute-done.13.refs_3_), channel_id=1, source_target_pairs={{0,8},{8,0},{16,24},{24,16},{1,9},{9,1},{17,25},{25,17},{2,10},{10... | collective-permute-start | bytes 1572872 | tf_op jit(solution)/shard_map/ppermute | solution.py:185
  153.6 1.9 copy-start.7
  161.5 1.9 collective-permute-start.15
  162.0 6.4 %collective-permute-start.16 = (bf16[256,256]{1,0:T(8,128)(2,1)S(1)}, bf16[256,256]{1,0:T(8,128)(2,1)S(1)}, u32[]{:S(2)}, u32[]{:S(2)}) collective-permute-start(bf16[256,256]{1,0:T(8,128)(2,1)S(1)} %get-tuple-element.36), channel_id=1, source_target_pairs={{0,16},{8,24},{16,0},{24,8},{1,17},{9,25},{17,1},{25,9},{2,18},{10... | collective-permute-start | bytes 393224 | tf_op jit(solution)/shard_map/ppermute | solution.py:185
  162.4 6.8 %collective-permute-start.17 = (bf16[256,256]{1,0:T(8,128)(2,1)S(1)}, bf16[256,256]{1,0:T(8,128)(2,1)S(1)}, u32[]{:S(2)}, u32[]{:S(2)}) collective-permute-start(bf16[256,256]{1,0:T(8,128)(2,1)S(1)} %get-tuple-element.37), channel_id=1, source_target_pairs={{0,24},{8,16},{16,8},{24,0},{1,25},{9,17},{17,9},{25,1},{2,26},{10... | collective-permute-start | bytes 393224 | tf_op jit(solution)/shard_map/ppermute | solution.py:185
  169.3 1.6 copy-start
  170.9 15.5 %copy-start.4 = (bf16[1024,2,512]{2,1,0:T(2,128)(2,1)S(1)}, bf16[1024,2,512]{2,1,0:T(2,128)(2,1)}, u32[]{:S(2)}) copy-start(bf16[1024,2,512]{2,1,0:T(2,128)(2,1)} %param.12) | copy-start | bytes 6291460
  171.7 14.7 %collective-permute-start.19 = (bf16[256,1024]{1,0:T(8,128)(2,1)S(1)}, bf16[256,1024]{1,0:T(8,128)(2,1)S(1)}, u32[]{:S(2)}, u32[]{:S(2)}) collective-permute-start(bf16[256,1024]{1,0:T(8,128)(2,1)S(1)} %get-tuple-element.39.refs_0_), channel_id=1, source_target_pairs={{0,16},{8,24},{16,0},{24,8},{1,17},{9,25},{17,1},{25,9},{2,18},{10... | collective-permute-start | bytes 1572872 | tf_op jit(solution)/shard_map/ppermute | solution.py:185
  172.4 14.6 %collective-permute-start.18 = (bf16[256,1024]{1,0:T(8,128)(2,1)S(1)}, bf16[256,1024]{1,0:T(8,128)(2,1)S(1)}, u32[]{:S(2)}, u32[]{:S(2)}) collective-permute-start(bf16[256,1024]{1,0:T(8,128)(2,1)S(1)} %get-tuple-element.39.refs_0_), channel_id=1, source_target_pairs={{0,8},{8,0},{16,24},{24,16},{1,9},{9,1},{17,25},{25,17},{2,10},{10... | collective-permute-start | bytes 1572872 | tf_op jit(solution)/shard_map/ppermute | solution.py:185
  186.4 1.9 collective-permute-start.20
  190.7 1.9 collective-permute-start.21
  190.9 9.2 %collective-permute-start.22 = (bf16[256,512]{1,0:T(8,128)(2,1)S(1)}, bf16[256,512]{1,0:T(8,128)(2,1)S(1)}, u32[]{:S(2)}, u32[]{:S(2)}) collective-permute-start(bf16[256,512]{1,0:T(8,128)(2,1)S(1)} %get-tuple-element.42), channel_id=1, source_target_pairs={{0,16},{8,24},{16,0},{24,8},{1,17},{9,25},{17,1},{25,9},{2,18},{10... | collective-permute-start | bytes 786440 | tf_op jit(solution)/shard_map/ppermute | solution.py:185
  191.3 13.2 %collective-permute-start.23 = (bf16[256,512]{1,0:T(8,128)(2,1)S(1)}, bf16[256,512]{1,0:T(8,128)(2,1)S(1)}, u32[]{:S(2)}, u32[]{:S(2)}) collective-permute-start(bf16[256,512]{1,0:T(8,128)(2,1)S(1)} %get-tuple-element.43), channel_id=1, source_target_pairs={{0,24},{8,16},{16,8},{24,0},{1,25},{9,17},{17,9},{25,1},{2,26},{10... | collective-permute-start | bytes 786440 | tf_op jit(solution)/shard_map/ppermute | solution.py:185
  209.6 12.7 %collective-permute-start.24 = (bf16[1,64,1024]{2,0,1:T(2,128)(2,1)S(1)}, bf16[1,64,1024]{2,0,1:T(2,128)(2,1)S(1)}, u32[]{:S(2)}, u32[]{:S(2)}) collective-permute-start(bf16[1,64,1024]{2,0,1:T(2,128)(2,1)S(1)} %get-tuple-element.53), channel_id=1, source_target_pairs={{0,2},{2,0},{4,6},{6,4},{1,3},{3,1},{5,7},{7,5},{8,10},{10,8},{12,... | collective-permute-start | bytes 393224 | tf_op jit(solution)/shard_map/ppermute | solution.py:247
  209.7 21.4 %collective-permute-start.25 = (bf16[1,64,1024]{2,0,1:T(2,128)(2,1)S(1)}, bf16[1,64,1024]{2,0,1:T(2,128)(2,1)S(1)}, u32[]{:S(2)}, u32[]{:S(2)}) collective-permute-start(bf16[1,64,1024]{2,0,1:T(2,128)(2,1)S(1)} %get-tuple-element.52), channel_id=1, source_target_pairs={{0,4},{2,6},{4,0},{6,2},{1,5},{3,7},{5,1},{7,3},{8,12},{10,14},{12... | collective-permute-start | bytes 393224 | tf_op jit(solution)/shard_map/ppermute | solution.py:247
  209.8 23.1 %collective-permute-start.26 = (bf16[1,64,1024]{2,0,1:T(2,128)(2,1)S(1)}, bf16[1,64,1024]{2,0,1:T(2,128)(2,1)S(1)}, u32[]{:S(2)}, u32[]{:S(2)}) collective-permute-start(bf16[1,64,1024]{2,0,1:T(2,128)(2,1)S(1)} %get-tuple-element.51), channel_id=1, source_target_pairs={{0,6},{2,4},{4,2},{6,0},{1,7},{3,5},{5,3},{7,1},{8,14},{10,12},{12... | collective-permute-start | bytes 393224 | tf_op jit(solution)/shard_map/ppermute | solution.py:247
Sparse Core Ops, SparseCore 0:
  9.2 30.6 all-gather.5
  41.5 25.5 all-gather.7
  68.7 22.5 all-gather.9
  92.7 42.3 all-gather.11
